TPU v7x, 512 devices: a whole 4x8x8 slice. The times are simulated.
512 devices in a mesh: sub: 16 (over z, core), dom: 32 (over y, x).
Axes of the slice: x: 4, y: 8, z: 8, core: 2. Of those that a mesh axis runs over, the one named last changes fastest.
Arguments:
- leaf_maps: bfloat16 [32, 16, 512, 512], P('dom', 'sub'), may hold values from -0.1875 to 0.1875
- edge_blocks: int32 [32, 16], P('dom'), may hold values from 0 to 15, each once within a row
- incoming: float32 [32, 16, 512, 256], P('dom', 'sub'), may hold values from -6 to 6
Outputs:
- parent_maps: bfloat16 [32, 16, 2048, 512], P('dom', 'sub')
- leaf_traces: float32 [32, 16, 512, 256], P('dom', 'sub')
Inputs may be any that keep to these rules, and one draw needn't show every extreme that they name: `edge_blocks`: each row is a permutation of the 16 blocks.
All inputs are finite; a program needn't handle non-finite values.
Results may differ from a plain program's by a relative error of at most 0.0085.
Values may be sent and summed in bfloat16 or wider, within the bound.
No kernel may reach another device: no remote copies, remote signals or barrier semaphores. Data moves between devices by JAX's collectives and lax.ppermute only.
A program may use at most 64 MiB of HBM per device.

v0:
```python
import jax
import jax.numpy as jnp
from jax import lax
from jax.experimental import pallas as pl
from jax.experimental.pallas import tpu as pltpu
from jax.sharding import PartitionSpec as P


KTERMS = 4
EDGE = 128
NT = (((1,), (1,)), ((), ()))
BF16 = jnp.bfloat16
F32 = jnp.float32
VMEM = pl.BlockSpec(memory_space=pltpu.VMEM)
EMPTY = pltpu.VMEM((8, 128), F32)
SMEM = pl.BlockSpec(memory_space=pltpu.SMEM)


def near(value):
    return pltpu.with_memory_space_constraint(value, pltpu.VMEM)


def call(kernel, results, args, scratch=(), edge=None):
    specs = [VMEM] * len(args)
    args = list(args)
    if edge is not None:
        specs, args = [SMEM] + specs, [edge] + args
    many = isinstance(results, tuple)
    made = pl.pallas_call(
        kernel,
        out_shape=results,
        in_specs=specs,
        out_specs=(VMEM,) * len(results) if many else VMEM,
        scratch_shapes=list(scratch),
        compiler_params=pltpu.CompilerParams(vmem_limit_bytes=16 << 20),
    )(*args)
    if many:
        return tuple(near(m) for m in made)
    return near(made) if isinstance(results, type(EMPTY)) else made


def sub_partner(value, mask):
    size = lax.axis_size("sub")
    return near(lax.ppermute(value, "sub", [(i, i ^ mask) for i in range(size)]))


def dom_partner(value, first):
    size = lax.axis_size("dom")
    pairs = []
    for low in range(first, first + size, 2):
        left, right = low % size, (low + 1) % size
        pairs += [(left, right), (right, left)]
    return near(lax.ppermute(value, "dom", pairs))


def split_kernel(edge_ref, own_ref, x_ref, edge_out, own_out, *refs):
    piece_refs, sem = refs[:4], refs[4]
    copy = pltpu.make_async_copy(own_ref, own_out, sem)
    copy.start()
    for k in range(edge_ref.shape[1]):
        edge_out[0, k] = edge_ref[0, k]
    position = lax.axis_index("sub") % 4
    turned = x_ref[...].T.astype(BF16)
    width = turned.shape[0] // 4
    for index in range(4):
        block = turned[index * width : (index + 1) * width]
        for r, piece in enumerate(piece_refs):
            @pl.when((position ^ r) == index)
            def _():
                for i in range(4):
                    piece[i] = block[:, i * EDGE : (i + 1) * EDGE]
    copy.wait()


def split_rhs(edge, own, x):
    rows, cols = x.shape
    piece = pltpu.VMEM((rows // EDGE, cols // 4, EDGE), BF16)
    edge, own, *pieces = pl.pallas_call(
        split_kernel,
        out_shape=(pltpu.SMEM(edge.shape, jnp.int32), pltpu.VMEM(own.shape, BF16)) + (piece,) * 4,
        in_specs=[SMEM, pl.BlockSpec(memory_space=pl.ANY), VMEM],
        out_specs=(SMEM,) + (VMEM,) * 5,
        scratch_shapes=[pltpu.SemaphoreType.DMA],
        compiler_params=pltpu.CompilerParams(vmem_limit_bytes=16 << 20),
    )(edge, own, x)
    edge = pltpu.with_memory_space_constraint(edge, pltpu.SMEM)
    return edge, near(own), [near(p) for p in pieces]


def swapped_in(given_refs, got_a, got_b, parity):
    def block(r, i):
        half, k = i // 2, i % 2
        a, b = got_a[r, k].astype(F32), got_b[r, k].astype(F32)
        even_pick = b if half == 0 else a
        odd_pick = a if half == 0 else b
        return given_refs[r][i].astype(F32) + jnp.where(parity == 0, even_pick, odd_pick)

    return block


def chain(edge_ref, turned, base_block, store, z_ref):
    position = lax.axis_index("sub") % 4
    for step in range(KTERMS + 1):
        slot, before = step % 2, (step + 1) % 2
        for r in range(4):
            leaf = position ^ r
            parts = []
            for i in range(4):
                part = base_block(r, i)
                if step > 0:
                    part = part + z_ref[before, edge_ref[0, leaf * 4 + i]]
                parts.append(part.astype(BF16))
            operand = jnp.concatenate(parts, 1)
            out = jnp.dot(operand, turned[r], preferred_element_type=F32)
            for i in range(4):
                value = out[:, i * EDGE : (i + 1) * EDGE]
                if step == KTERMS:
                    store(r, i, value)
                else:
                    z_ref[slot, leaf * 4 + i] = value


def send_store(to_a, to_b, parity):
    def store(r, i, value):
        half, k = i // 2, i % 2
        value = value.astype(BF16)

        @pl.when(parity == half)
        def _():
            to_b[r, k] = value

        @pl.when(parity != half)
        def _():
            to_a[r, k] = value

    return store


def first_sweep_kernel(edge, m0, m1, m2, m3, g0, g1, g2, g3, to_a, to_b, turned, z):
    parity = lax.axis_index("dom") % 2
    given = (g0, g1, g2, g3)
    for r, m in enumerate((m0, m1, m2, m3)):
        turned[r] = m[...].T
    chain(
        edge, turned, lambda r, i: given[r][i].astype(F32), send_store(to_a, to_b, parity), z
    )


def next_sweep_kernel(edge, turned, g0, g1, g2, g3, got_a, got_b, to_a, to_b, v, z):
    parity = lax.axis_index("dom") % 2
    block = swapped_in((g0, g1, g2, g3), got_a, got_b, parity)
    for r in range(4):
        for i in range(4):
            v[r, i] = block(r, i).astype(BF16)
    chain(
        edge, turned, lambda r, i: v[r, i].astype(F32), send_store(to_a, to_b, parity), z
    )


def first_sweep(edge, maps, given):
    blocks, width, _ = given[0].shape
    sent = pltpu.VMEM((4, blocks // 2, width, EDGE), BF16)
    turned = pltpu.VMEM((4,) + maps[0].shape, BF16)
    z = pltpu.VMEM((2, 4 * blocks, width, EDGE), F32)
    return call(first_sweep_kernel, (sent, sent, turned), (*maps, *given), (z,), edge)


def next_sweep(edge, turned, given, got):
    blocks, width, _ = given[0].shape
    sent = pltpu.VMEM((4, blocks // 2, width, EDGE), BF16)
    v = pltpu.VMEM((4, blocks, width, EDGE), BF16)
    z = pltpu.VMEM((2, 4 * blocks, width, EDGE), F32)
    return call(next_sweep_kernel, (sent, sent), (turned, *given, *got), (v, z), edge)


def join_kernel(g0, g1, g2, g3, got_a, got_b, *out_refs):
    parity = lax.axis_index("dom") % 2
    block = swapped_in((g0, g1, g2, g3), got_a, got_b, parity)
    for r in range(4):
        for i in range(4):
            out_refs[r][i] = block(r, i).astype(BF16)


def join(given, got):
    return call(join_kernel, (pltpu.VMEM(given[0].shape, BF16),) * 4, (*given, *got))


def leaf_kernel(own, u0, u1, u2, u3, out, turned):
    position = lax.axis_index("sub") % 4
    width = u0.shape[1]
    for r, u in enumerate((u0, u1, u2, u3)):
        rows = pl.ds(pl.multiple_of((position ^ r) * width, width), width)
        for i in range(4):
            turned[rows, i * EDGE : (i + 1) * EDGE] = u[i]
    out[...] = lax.dot_general(own[...], turned[...], NT, preferred_element_type=F32)


def leaf_product(own, pieces):
    blocks, width, _ = pieces[0].shape
    result = jax.ShapeDtypeStruct((own.shape[0], 4 * width), F32)
    turned = pltpu.VMEM((4 * width, blocks * EDGE), BF16)
    return call(leaf_kernel, result, (own, *pieces), (turned,))


def apply_once(edge_ref, map_refs, source, target):
    position = lax.axis_index("sub") % 4
    for r in range(4):
        leaf = position ^ r
        operand = jnp.concatenate([source[edge_ref[0, leaf * 4 + i]] for i in range(4)], 0)
        out = jnp.dot(map_refs[r][...], operand, preferred_element_type=F32)
        if r == 0:
            out = out + map_refs[0][...].astype(F32)
        for i in range(4):
            target[leaf * 4 + i] = out[i * EDGE : (i + 1) * EDGE].astype(BF16)


def merge_first_kernel(edge, m0, m1, m2, m3, out, work):
    position = lax.axis_index("sub") % 4
    out[...] = jnp.zeros_like(out)
    for i in range(4):
        out[position * 4 + i] = m0[i * EDGE : (i + 1) * EDGE]
    apply_once(edge, (m0, m1, m2, m3), out, work)
    apply_once(edge, (m0, m1, m2, m3), work, out)


def merge_next_kernel(edge, m0, m1, m2, m3, source, out, work):
    apply_once(edge, (m0, m1, m2, m3), source, work)
    apply_once(edge, (m0, m1, m2, m3), work, out)


def merge(edge, maps, source):
    width = maps[0].shape[0]
    shape = (4 * width // EDGE, EDGE, width)
    work = pltpu.VMEM(shape, BF16)
    if source is None:
        return call(merge_first_kernel, work, maps, (work,), edge)
    result = jax.ShapeDtypeStruct(shape, BF16)
    return call(merge_next_kernel, result, (*maps, source), (work,), edge)


def per_device(leaf_maps, edge, incoming):
    return steps(leaf_maps[0, 0], edge, incoming[0, 0])


def steps(own, edge, incoming):
    width = own.shape[0]
    across = sub_partner(own, 2)
    edge, own_near, mine = split_rhs(edge, own, near(incoming))
    given = [mine[0]]
    beside = sub_partner(own, 1)
    for r in (1, 2, 3):
        given.append(sub_partner(mine[r], r))
    opposite = sub_partner(across, 1)
    maps = (own_near, beside, across, opposite)

    def swap(sent):
        far = dom_partner(sent[1], 1)
        return dom_partner(sent[0], 0), far

    *sent, turned = first_sweep(edge, maps, given)
    got = swap(sent)
    half_merged = merge(edge, maps, None)
    sent = next_sweep(edge, turned, given, got)
    got = swap(sent)
    merged = merge(edge, maps, half_merged)
    mine = join(given, got)
    pieces = [mine[0]]
    for r in (1, 2, 3):
        pieces.append(sub_partner(mine[r], r))
    leaf_out = leaf_product(own_near, pieces)
    return merged.reshape(1, 1, 4 * width, width), leaf_out[None, None]


def solution(mesh):
    placed = (P("dom", "sub", None, None), P("dom", None), P("dom", "sub", None, None))
    return jax.shard_map(
        per_device,
        mesh=mesh,
        in_specs=placed,
        out_specs=(P("dom", "sub", None, None), P("dom", "sub", None, None)),
        check_vma=False,
    )
```

profile of v0, /device:TPU:1, one launch (start us, length us, event | category | flops | bytes accessed | tf_op | source)
XLA Modules:
  0.0 84.6 jit_solution(12801301175561318005)
XLA Ops:
  0.6 4.8 %collective-permute-start.1 = (bf16[512,512]{1,0:T(8,128)(2,1)}, bf16[512,512]{1,0:T(8,128)(2,1)S(1)}, u32[]{:S(2)}, u32[]{:S(2)}) collective-permute-start(bf16[512,512]{1,0:T(8,128)(2,1)} %bitcast.5), channel_id=1, source_target_pairs={{0,64},{32,96},{64,0},{96,32},{128,192},{160,224},{192,128},{224,1... | collective-permute-start | bytes 1572872 | tf_op jit(solution)/shard_map/ppermute | solution.py:44
  5.5 5.8 %collective-permute-start = (bf16[512,512]{1,0:T(8,128)(2,1)}, bf16[512,512]{1,0:T(8,128)(2,1)S(1)}, u32[]{:S(2)}, u32[]{:S(2)}) collective-permute-start(bf16[512,512]{1,0:T(8,128)(2,1)} %bitcast.6), channel_id=1, source_target_pairs={{0,32},{32,0},{64,96},{96,64},{128,160},{160,128},{192,224},{224,1... | collective-permute-start | bytes 1572872 | tf_op jit(solution)/shard_map/ppermute | solution.py:44
  11.3 2.1 %collective-permute-done.1.m2 = bf16[512,512]{1,0:T(8,128)(2,1)S(1)} collective-permute-done((bf16[512,512]{1,0:T(8,128)(2,1)}, bf16[512,512]{1,0:T(8,128)(2,1)S(1)}, u32[]{:S(2)}, u32[]{:S(2)}) %collective-permute-start.1) | collective-permute-done | bytes 524320 | tf_op jit(solution)/shard_map/ppermute | solution.py:44
  13.4 7.3 %collective-permute-start.2 = (bf16[512,512]{1,0:T(8,128)(2,1)S(1)}, bf16[512,512]{1,0:T(8,128)(2,1)S(1)}, u32[]{:S(2)}, u32[]{:S(2)}) collective-permute-start(bf16[512,512]{1,0:T(8,128)(2,1)S(1)} %collective-permute-done.1.m2), channel_id=1, source_target_pairs={{0,32},{32,0},{64,96},{96,64},{128,160},{160,128},{192,224},{224,1... | collective-permute-start | bytes 1572872 | tf_op jit(solution)/shard_map/ppermute | solution.py:44
  20.7 0.0 copy-start
  20.7 1.0 %copy-done = f32[1,1,512,256]{3,2,1,0:T(8,128)S(1)} copy-done((f32[1,1,512,256]{3,2,1,0:T(8,128)S(1)}, f32[1,1,512,256]{3,2,1,0:T(8,128)}, u32[]{:S(2)}) %copy-start) | copy-done | bytes 524312
  21.7 0.0 copy-start.1
  21.7 1.0 %copy-done.1 = bf16[1,1,512,512]{3,2,1,0:T(8,128)(2,1)S(1)} copy-done((bf16[1,1,512,512]{3,2,1,0:T(8,128)(2,1)S(1)}, bf16[1,1,512,512]{3,2,1,0:T(8,128)(2,1)}, u32[]{:S(2)}) %copy-start.1) | copy-done | bytes 524312
  22.7 0.0 copy-start.2
  22.7 0.7 copy-done.2
  23.4 0.8 shard_map.50
  24.2 1.9 %collective-permute-start.3 = (bf16[4,64,128]{2,1,0:T(8,128)(2,1)S(1)}, bf16[4,64,128]{2,1,0:T(8,128)(2,1)S(1)}, u32[]{:S(2)}, u32[]{:S(2)}) collective-permute-start(bf16[4,64,128]{2,1,0:T(8,128)(2,1)S(1)} %get-tuple-element.20), channel_id=1, source_target_pairs={{0,32},{32,0},{64,96},{96,64},{128,160},{160,128},{192,224},{224,1... | collective-permute-start | bytes 196616 | tf_op jit(solution)/shard_map/ppermute | solution.py:44
  26.1 3.1 %collective-permute-start.4 = (bf16[4,64,128]{2,1,0:T(8,128)(2,1)S(1)}, bf16[4,64,128]{2,1,0:T(8,128)(2,1)S(1)}, u32[]{:S(2)}, u32[]{:S(2)}) collective-permute-start(bf16[4,64,128]{2,1,0:T(8,128)(2,1)S(1)} %get-tuple-element.21), channel_id=1, source_target_pairs={{0,64},{32,96},{64,0},{96,32},{128,192},{160,224},{192,128},{224,1... | collective-permute-start | bytes 196616 | tf_op jit(solution)/shard_map/ppermute | solution.py:44
  29.3 2.8 %collective-permute-start.5 = (bf16[4,64,128]{2,1,0:T(8,128)(2,1)S(1)}, bf16[4,64,128]{2,1,0:T(8,128)(2,1)S(1)}, u32[]{:S(2)}, u32[]{:S(2)}) collective-permute-start(bf16[4,64,128]{2,1,0:T(8,128)(2,1)S(1)} %get-tuple-element.22), channel_id=1, source_target_pairs={{0,96},{32,64},{64,32},{96,0},{128,224},{160,192},{192,160},{224,1... | collective-permute-start | bytes 196616 | tf_op jit(solution)/shard_map/ppermute | solution.py:44
  32.1 0.0 collective-permute-done.3.g1
  32.1 0.0 collective-permute-done.4.g2
  32.1 3.7 %collective-permute-done.5.g3 = bf16[4,64,128]{2,1,0:T(8,128)(2,1)S(1)} collective-permute-done((bf16[4,64,128]{2,1,0:T(8,128)(2,1)S(1)}, bf16[4,64,128]{2,1,0:T(8,128)(2,1)S(1)}, u32[]{:S(2)}, u32[]{:S(2)}) %collective-permute-start.5) | collective-permute-done | bytes 65568 | tf_op jit(solution)/shard_map/ppermute | solution.py:44
  35.8 0.0 collective-permute-done.m1
  35.8 0.0 collective-permute-done.2.m3
  35.8 3.8 %shard_map.53 = (bf16[4,2,64,128]{3,2,1,0:T(8,128)(2,1)S(1)}, bf16[4,2,64,128]{3,2,1,0:T(8,128)(2,1)S(1)}, bf16[4,512,512]{2,1,0:T(8,128)(2,1)S(1)}) custom-call(s32[1,16]{1,0:T(1,128)S(4)} %get-tuple-element.17.edge, bf16[512,512]{1,0:T(8,128)(2,1)S(1)} %get-tuple-element.18.m0.own, bf16[512,512]{1,0:T(8,128)(2,1)S(1)} %collective-permute-done.m1, ...), custom_call_target="tpu_custom_call" | custom-call | tf_op jit(solution)/shard_map/pallas_call | solution.py:29
  39.5 3.1 %collective-permute-start.6 = (bf16[4,2,64,128]{3,2,1,0:T(8,128)(2,1)S(1)}, bf16[4,2,64,128]{3,2,1,0:T(8,128)(2,1)S(1)}, u32[]{:S(2)}, u32[]{:S(2)}) collective-permute-start(bf16[4,2,64,128]{3,2,1,0:T(8,128)(2,1)S(1)} %get-tuple-element.24), channel_id=1, source_target_pairs={{0,1},{1,0},{2,3},{3,2},{4,5},{5,4},{6,7},{7,6},{8,9},{9,8},{10,11... | collective-permute-start | bytes 393224 | tf_op jit(solution)/shard_map/ppermute | solution.py:53
  42.6 6.7 %collective-permute-start.7 = (bf16[4,2,64,128]{3,2,1,0:T(8,128)(2,1)S(1)}, bf16[4,2,64,128]{3,2,1,0:T(8,128)(2,1)S(1)}, u32[]{:S(2)}, u32[]{:S(2)}) collective-permute-start(bf16[4,2,64,128]{3,2,1,0:T(8,128)(2,1)S(1)} %get-tuple-element.25), channel_id=1, source_target_pairs={{1,2},{2,1},{3,4},{4,3},{5,6},{6,5},{7,8},{8,7},{9,10},{10,9},{11,... | collective-permute-start | bytes 393224 | tf_op jit(solution)/shard_map/ppermute | solution.py:53
  49.3 0.0 collective-permute-done.6.got_a
  49.3 2.8 %collective-permute-done.7.got_b = bf16[4,2,64,128]{3,2,1,0:T(8,128)(2,1)S(1)} collective-permute-done((bf16[4,2,64,128]{3,2,1,0:T(8,128)(2,1)S(1)}, bf16[4,2,64,128]{3,2,1,0:T(8,128)(2,1)S(1)}, u32[]{:S(2)}, u32[]{:S(2)}) %collective-permute-start.7) | collective-permute-done | bytes 131104 | tf_op jit(solution)/shard_map/ppermute | solution.py:53
  52.1 3.5 %shard_map.54 = (bf16[4,2,64,128]{3,2,1,0:T(8,128)(2,1)S(1)}, bf16[4,2,64,128]{3,2,1,0:T(8,128)(2,1)S(1)}) custom-call(s32[1,16]{1,0:T(1,128)S(4)} %get-tuple-element.17.edge, bf16[4,512,512]{2,1,0:T(8,128)(2,1)S(1)} %get-tuple-element.23.turned, bf16[4,64,128]{2,1,0:T(8,128)(2,1)S(1)} %get-tuple-element.19.g0, ...), custom_call_target="tpu_custom_call" | custom-call | tf_op jit(solution)/shard_map/pallas_call | solution.py:29
  55.7 1.9 %collective-permute-start.8 = (bf16[4,2,64,128]{3,2,1,0:T(8,128)(2,1)S(1)}, bf16[4,2,64,128]{3,2,1,0:T(8,128)(2,1)S(1)}, u32[]{:S(2)}, u32[]{:S(2)}) collective-permute-start(bf16[4,2,64,128]{3,2,1,0:T(8,128)(2,1)S(1)} %get-tuple-element.26), channel_id=1, source_target_pairs={{0,1},{1,0},{2,3},{3,2},{4,5},{5,4},{6,7},{7,6},{8,9},{9,8},{10,11... | collective-permute-start | bytes 393224 | tf_op jit(solution)/shard_map/ppermute | solution.py:53
  57.6 6.6 %collective-permute-start.9 = (bf16[4,2,64,128]{3,2,1,0:T(8,128)(2,1)S(1)}, bf16[4,2,64,128]{3,2,1,0:T(8,128)(2,1)S(1)}, u32[]{:S(2)}, u32[]{:S(2)}) collective-permute-start(bf16[4,2,64,128]{3,2,1,0:T(8,128)(2,1)S(1)} %get-tuple-element.27), channel_id=1, source_target_pairs={{1,2},{2,1},{3,4},{4,3},{5,6},{6,5},{7,8},{8,7},{9,10},{10,9},{11,... | collective-permute-start | bytes 393224 | tf_op jit(solution)/shard_map/ppermute | solution.py:53
  64.2 0.0 collective-permute-done.8.got_a
  64.2 2.4 %collective-permute-done.9.got_b = bf16[4,2,64,128]{3,2,1,0:T(8,128)(2,1)S(1)} collective-permute-done((bf16[4,2,64,128]{3,2,1,0:T(8,128)(2,1)S(1)}, bf16[4,2,64,128]{3,2,1,0:T(8,128)(2,1)S(1)}, u32[]{:S(2)}, u32[]{:S(2)}) %collective-permute-start.9) | collective-permute-done | bytes 131104 | tf_op jit(solution)/shard_map/ppermute | solution.py:53
  66.6 0.1 shard_map.55
  66.7 4.7 %collective-permute-start.10 = (bf16[4,64,128]{2,1,0:T(8,128)(2,1)S(1)}, bf16[4,64,128]{2,1,0:T(8,128)(2,1)S(1)}, u32[]{:S(2)}, u32[]{:S(2)}) collective-permute-start(bf16[4,64,128]{2,1,0:T(8,128)(2,1)S(1)} %get-tuple-element.29), channel_id=1, source_target_pairs={{0,32},{32,0},{64,96},{96,64},{128,160},{160,128},{192,224},{224,1... | collective-permute-start | bytes 196616 | tf_op jit(solution)/shard_map/ppermute | solution.py:44
  71.4 1.9 %collective-permute-start.11 = (bf16[4,64,128]{2,1,0:T(8,128)(2,1)S(1)}, bf16[4,64,128]{2,1,0:T(8,128)(2,1)S(1)}, u32[]{:S(2)}, u32[]{:S(2)}) collective-permute-start(bf16[4,64,128]{2,1,0:T(8,128)(2,1)S(1)} %get-tuple-element.30), channel_id=1, source_target_pairs={{0,64},{32,96},{64,0},{96,32},{128,192},{160,224},{192,128},{224,1... | collective-permute-start | bytes 196616 | tf_op jit(solution)/shard_map/ppermute | solution.py:44
  73.3 3.5 %collective-permute-start.12 = (bf16[4,64,128]{2,1,0:T(8,128)(2,1)S(1)}, bf16[4,64,128]{2,1,0:T(8,128)(2,1)S(1)}, u32[]{:S(2)}, u32[]{:S(2)}) collective-permute-start(bf16[4,64,128]{2,1,0:T(8,128)(2,1)S(1)} %get-tuple-element.31), channel_id=1, source_target_pairs={{0,96},{32,64},{64,32},{96,0},{128,224},{160,192},{192,160},{224,1... | collective-permute-start | bytes 196616 | tf_op jit(solution)/shard_map/ppermute | solution.py:44
  76.9 2.7 %shard_map.51.source = bf16[16,128,512]{2,1,0:T(8,128)(2,1)S(1)} custom-call(s32[1,16]{1,0:T(1,128)S(4)} %get-tuple-element.17.edge, bf16[512,512]{1,0:T(8,128)(2,1)S(1)} %get-tuple-element.18.m0.own, bf16[512,512]{1,0:T(8,128)(2,1)S(1)} %collective-permute-done.m1, bf16[512,512]{1,0:T(8,128)(2,1)S(1)} %collective-permute-done.1.m2, ...), custom_call_target="tpu_custom_call" | custom-call | tf_op jit(solution)/shard_map/pallas_call | solution.py:29
  79.6 3.9 %shard_map.52 = bf16[16,128,512]{2,1,0:T(8,128)(2,1)} custom-call(s32[1,16]{1,0:T(1,128)S(4)} %get-tuple-element.17.edge, bf16[512,512]{1,0:T(8,128)(2,1)S(1)} %get-tuple-element.18.m0.own, bf16[512,512]{1,0:T(8,128)(2,1)S(1)} %collective-permute-done.m1, bf16[512,512]{1,0:T(8,128)(2,1)S(1)} %collective-permute-done.1.m2, ...), custom_call_target="tpu_custom_call" | custom-call | tf_op jit(solution)/shard_map/pallas_call | solution.py:29
  83.4 0.0 collective-permute-done.10.u1
  83.4 0.0 collective-permute-done.11.u2
  83.4 0.0 collective-permute-done.12.u3
  83.4 1.2 %shard_map.56 = f32[512,256]{1,0:T(8,128)} custom-call(bf16[512,512]{1,0:T(8,128)(2,1)S(1)} %get-tuple-element.18.m0.own, bf16[4,64,128]{2,1,0:T(8,128)(2,1)S(1)} %get-tuple-element.28.u0, bf16[4,64,128]{2,1,0:T(8,128)(2,1)S(1)} %collective-permute-done.10.u1, bf16[4,64,128]{2,1,0:T(8,128)(2,1)S(1)} %collective-permute-done.11.u2, ...), custom_call_target="tpu_custom_call" | custom-call | tf_op jit(solution)/shard_map/pallas_call | solution.py:29
Async XLA Ops:
  0.6 12.7 %collective-permute-start.1 = (bf16[512,512]{1,0:T(8,128)(2,1)}, bf16[512,512]{1,0:T(8,128)(2,1)S(1)}, u32[]{:S(2)}, u32[]{:S(2)}) collective-permute-start(bf16[512,512]{1,0:T(8,128)(2,1)} %bitcast.5), channel_id=1, source_target_pairs={{0,64},{32,96},{64,0},{96,32},{128,192},{160,224},{192,128},{224,1... | collective-permute-start | bytes 1572872 | tf_op jit(solution)/shard_map/ppermute | solution.py:44
  5.5 30.3 %collective-permute-start = (bf16[512,512]{1,0:T(8,128)(2,1)}, bf16[512,512]{1,0:T(8,128)(2,1)S(1)}, u32[]{:S(2)}, u32[]{:S(2)}) collective-permute-start(bf16[512,512]{1,0:T(8,128)(2,1)} %bitcast.6), channel_id=1, source_target_pairs={{0,32},{32,0},{64,96},{96,64},{128,160},{160,128},{192,224},{224,1... | collective-permute-start | bytes 1572872 | tf_op jit(solution)/shard_map/ppermute | solution.py:44
  13.4 22.4 %collective-permute-start.2 = (bf16[512,512]{1,0:T(8,128)(2,1)S(1)}, bf16[512,512]{1,0:T(8,128)(2,1)S(1)}, u32[]{:S(2)}, u32[]{:S(2)}) collective-permute-start(bf16[512,512]{1,0:T(8,128)(2,1)S(1)} %collective-permute-done.1.m2), channel_id=1, source_target_pairs={{0,32},{32,0},{64,96},{96,64},{128,160},{160,128},{192,224},{224,1... | collective-permute-start | bytes 1572872 | tf_op jit(solution)/shard_map/ppermute | solution.py:44
  20.7 1.0 %copy-start = (f32[1,1,512,256]{3,2,1,0:T(8,128)S(1)}, f32[1,1,512,256]{3,2,1,0:T(8,128)}, u32[]{:S(2)}) copy-start(f32[1,1,512,256]{3,2,1,0:T(8,128)} %param.5) | copy-start | bytes 1572868
  21.7 1.0 %copy-start.1 = (bf16[1,1,512,512]{3,2,1,0:T(8,128)(2,1)S(1)}, bf16[1,1,512,512]{3,2,1,0:T(8,128)(2,1)}, u32[]{:S(2)}) copy-start(bf16[1,1,512,512]{3,2,1,0:T(8,128)(2,1)} %param.3) | copy-start | bytes 1572868
  22.7 0.7 copy-start.2
  24.2 7.9 %collective-permute-start.3 = (bf16[4,64,128]{2,1,0:T(8,128)(2,1)S(1)}, bf16[4,64,128]{2,1,0:T(8,128)(2,1)S(1)}, u32[]{:S(2)}, u32[]{:S(2)}) collective-permute-start(bf16[4,64,128]{2,1,0:T(8,128)(2,1)S(1)} %get-tuple-element.20), channel_id=1, source_target_pairs={{0,32},{32,0},{64,96},{96,64},{128,160},{160,128},{192,224},{224,1... | collective-permute-start | bytes 196616 | tf_op jit(solution)/shard_map/ppermute | solution.py:44
  26.1 6.0 %collective-permute-start.4 = (bf16[4,64,128]{2,1,0:T(8,128)(2,1)S(1)}, bf16[4,64,128]{2,1,0:T(8,128)(2,1)S(1)}, u32[]{:S(2)}, u32[]{:S(2)}) collective-permute-start(bf16[4,64,128]{2,1,0:T(8,128)(2,1)S(1)} %get-tuple-element.21), channel_id=1, source_target_pairs={{0,64},{32,96},{64,0},{96,32},{128,192},{160,224},{192,128},{224,1... | collective-permute-start | bytes 196616 | tf_op jit(solution)/shard_map/ppermute | solution.py:44
  29.3 6.5 %collective-permute-start.5 = (bf16[4,64,128]{2,1,0:T(8,128)(2,1)S(1)}, bf16[4,64,128]{2,1,0:T(8,128)(2,1)S(1)}, u32[]{:S(2)}, u32[]{:S(2)}) collective-permute-start(bf16[4,64,128]{2,1,0:T(8,128)(2,1)S(1)} %get-tuple-element.22), channel_id=1, source_target_pairs={{0,96},{32,64},{64,32},{96,0},{128,224},{160,192},{192,160},{224,1... | collective-permute-start | bytes 196616 | tf_op jit(solution)/shard_map/ppermute | solution.py:44
  39.5 9.8 %collective-permute-start.6 = (bf16[4,2,64,128]{3,2,1,0:T(8,128)(2,1)S(1)}, bf16[4,2,64,128]{3,2,1,0:T(8,128)(2,1)S(1)}, u32[]{:S(2)}, u32[]{:S(2)}) collective-permute-start(bf16[4,2,64,128]{3,2,1,0:T(8,128)(2,1)S(1)} %get-tuple-element.24), channel_id=1, source_target_pairs={{0,1},{1,0},{2,3},{3,2},{4,5},{5,4},{6,7},{7,6},{8,9},{9,8},{10,11... | collective-permute-start | bytes 393224 | tf_op jit(solution)/shard_map/ppermute | solution.py:53
  42.6 9.5 %collective-permute-start.7 = (bf16[4,2,64,128]{3,2,1,0:T(8,128)(2,1)S(1)}, bf16[4,2,64,128]{3,2,1,0:T(8,128)(2,1)S(1)}, u32[]{:S(2)}, u32[]{:S(2)}) collective-permute-start(bf16[4,2,64,128]{3,2,1,0:T(8,128)(2,1)S(1)} %get-tuple-element.25), channel_id=1, source_target_pairs={{1,2},{2,1},{3,4},{4,3},{5,6},{6,5},{7,8},{8,7},{9,10},{10,9},{11,... | collective-permute-start | bytes 393224 | tf_op jit(solution)/shard_map/ppermute | solution.py:53
  55.7 8.6 %collective-permute-start.8 = (bf16[4,2,64,128]{3,2,1,0:T(8,128)(2,1)S(1)}, bf16[4,2,64,128]{3,2,1,0:T(8,128)(2,1)S(1)}, u32[]{:S(2)}, u32[]{:S(2)}) collective-permute-start(bf16[4,2,64,128]{3,2,1,0:T(8,128)(2,1)S(1)} %get-tuple-element.26), channel_id=1, source_target_pairs={{0,1},{1,0},{2,3},{3,2},{4,5},{5,4},{6,7},{7,6},{8,9},{9,8},{10,11... | collective-permute-start | bytes 393224 | tf_op jit(solution)/shard_map/ppermute | solution.py:53
  57.6 9.0 %collective-permute-start.9 = (bf16[4,2,64,128]{3,2,1,0:T(8,128)(2,1)S(1)}, bf16[4,2,64,128]{3,2,1,0:T(8,128)(2,1)S(1)}, u32[]{:S(2)}, u32[]{:S(2)}) collective-permute-start(bf16[4,2,64,128]{3,2,1,0:T(8,128)(2,1)S(1)} %get-tuple-element.27), channel_id=1, source_target_pairs={{1,2},{2,1},{3,4},{4,3},{5,6},{6,5},{7,8},{8,7},{9,10},{10,9},{11,... | collective-permute-start | bytes 393224 | tf_op jit(solution)/shard_map/ppermute | solution.py:53
  66.7 16.7 %collective-permute-start.10 = (bf16[4,64,128]{2,1,0:T(8,128)(2,1)S(1)}, bf16[4,64,128]{2,1,0:T(8,128)(2,1)S(1)}, u32[]{:S(2)}, u32[]{:S(2)}) collective-permute-start(bf16[4,64,128]{2,1,0:T(8,128)(2,1)S(1)} %get-tuple-element.29), channel_id=1, source_target_pairs={{0,32},{32,0},{64,96},{96,64},{128,160},{160,128},{192,224},{224,1... | collective-permute-start | bytes 196616 | tf_op jit(solution)/shard_map/ppermute | solution.py:44
  71.4 12.0 %collective-permute-start.11 = (bf16[4,64,128]{2,1,0:T(8,128)(2,1)S(1)}, bf16[4,64,128]{2,1,0:T(8,128)(2,1)S(1)}, u32[]{:S(2)}, u32[]{:S(2)}) collective-permute-start(bf16[4,64,128]{2,1,0:T(8,128)(2,1)S(1)} %get-tuple-element.30), channel_id=1, source_target_pairs={{0,64},{32,96},{64,0},{96,32},{128,192},{160,224},{192,128},{224,1... | collective-permute-start | bytes 196616 | tf_op jit(solution)/shard_map/ppermute | solution.py:44
  73.3 10.1 %collective-permute-start.12 = (bf16[4,64,128]{2,1,0:T(8,128)(2,1)S(1)}, bf16[4,64,128]{2,1,0:T(8,128)(2,1)S(1)}, u32[]{:S(2)}, u32[]{:S(2)}) collective-permute-start(bf16[4,64,128]{2,1,0:T(8,128)(2,1)S(1)} %get-tuple-element.31), channel_id=1, source_target_pairs={{0,96},{32,64},{64,32},{96,0},{128,224},{160,192},{192,160},{224,1... | collective-permute-start | bytes 196616 | tf_op jit(solution)/shard_map/ppermute | solution.py:44
where the time goes:
time: 85.2 us; the launch traced here: 84.6 us
  starting transfers between devices  54.3 us (64%)
  Pallas kernels  15.9 us (19%)
  waiting for transfers between devices  10.9 us (13%)
  local copies, waits for them, and re-layouts  2.73 us (3%)
    ppermute x9, starting transfers between devices, sub_partner(): lax.ppermute(value, 'sub', [(i, i ^ mask) for i in range(size)])  36 us
    ppermute x4, starting transfers between devices, dom_partner(): return near(lax.ppermute(value, 'dom', pairs))  18.3 us
    pallas_call x6, Pallas kernels, call(): pl.pallas_call(kernel, out_shape=results, in_specs=specs, out_specs=(VMEM...  15.1 us
    ppermute x9, waiting for transfers between devices, sub_partner(): lax.ppermute(value, 'sub', [(i, i ^ mask) for i in range(size)])  5.73 us
    ppermute x4, waiting for transfers between devices, dom_partner(): return near(lax.ppermute(value, 'dom', pairs))  5.2 us
    unnamed x6, local copies, waits for them, and re-layouts  2.73 us
  transfers between devices with their start and end apart: 13, of which 4 were waited for; matrix products, arithmetic and copies ran while one was open for 0% of the time, Pallas kernels for 9%

commit v1 on v0

--- a/solution.py
+++ b/solution.py
@@ -53,47 +53,56 @@
     return near(lax.ppermute(value, "dom", pairs))
 
 
-def split_kernel(edge_ref, own_ref, x_ref, edge_out, own_out, *refs):
-    piece_refs, sem = refs[:4], refs[4]
-    copy = pltpu.make_async_copy(own_ref, own_out, sem)
-    copy.start()
-    for k in range(edge_ref.shape[1]):
-        edge_out[0, k] = edge_ref[0, k]
-    position = lax.axis_index("sub") % 4
+def group_exchange(value):
+    size = lax.axis_size("sub")
+    groups = [list(range(g, g + 4)) for g in range(0, size, 4)]
+    return near(lax.all_to_all(value, "sub", 0, 0, axis_index_groups=groups))
+
+
+def split_kernel(edge_in, own_in, x_in, edge_out, own_out, pieces, x_ref, sems):
+    fetch = pltpu.make_async_copy(x_in, x_ref, sems.at[0])
+    others = [
+        pltpu.make_async_copy(edge_in, edge_out, sems.at[1]),
+        pltpu.make_async_copy(own_in, own_out, sems.at[2]),
+    ]
+    for copy in [fetch] + others:
+        copy.start()
+    fetch.wait()
     turned = x_ref[...].T.astype(BF16)
     width = turned.shape[0] // 4
-    for index in range(4):
-        block = turned[index * width : (index + 1) * width]
-        for r, piece in enumerate(piece_refs):
-            @pl.when((position ^ r) == index)
-            def _():
-                for i in range(4):
-                    piece[i] = block[:, i * EDGE : (i + 1) * EDGE]
-    copy.wait()
+    for k in range(4):
+        for i in range(4):
+            pieces[k, i] = turned[k * width : (k + 1) * width, i * EDGE : (i + 1) * EDGE]
+    for copy in others:
+        copy.wait()
 
 
 def split_rhs(edge, own, x):
     rows, cols = x.shape
-    piece = pltpu.VMEM((rows // EDGE, cols // 4, EDGE), BF16)
-    edge, own, *pieces = pl.pallas_call(
+    edge, own, pieces = pl.pallas_call(
         split_kernel,
-        out_shape=(pltpu.SMEM(edge.shape, jnp.int32), pltpu.VMEM(own.shape, BF16)) + (piece,) * 4,
-        in_specs=[SMEM, pl.BlockSpec(memory_space=pl.ANY), VMEM],
-        out_specs=(SMEM,) + (VMEM,) * 5,
-        scratch_shapes=[pltpu.SemaphoreType.DMA],
+        out_shape=(
+            pltpu.SMEM(edge.shape, jnp.int32),
+            pltpu.VMEM(own.shape, BF16),
+            pltpu.VMEM((4, rows // EDGE, cols // 4, EDGE), BF16),
+        ),
+        in_specs=[pl.BlockSpec(memory_space=pltpu.HBM)] * 3,
+        out_specs=(SMEM, VMEM, VMEM),
+        scratch_shapes=[pltpu.VMEM(x.shape, F32), pltpu.SemaphoreType.DMA((3,))],
         compiler_params=pltpu.CompilerParams(vmem_limit_bytes=16 << 20),
-    )(edge, own, x)
-    edge = pltpu.with_memory_space_constraint(edge, pltpu.SMEM)
-    return edge, near(own), [near(p) for p in pieces]
-
-
-def swapped_in(given_refs, got_a, got_b, parity):
+    )(*(pltpu.with_memory_space_constraint(a, pltpu.HBM) for a in (edge, own, x)))
+    return pltpu.with_memory_space_constraint(edge, pltpu.SMEM), near(own), near(pieces)
+
+
+def swapped_in(given, got_a, got_b):
+    position, parity = lax.axis_index("sub") % 4, lax.axis_index("dom") % 2
+
     def block(r, i):
         half, k = i // 2, i % 2
         a, b = got_a[r, k].astype(F32), got_b[r, k].astype(F32)
         even_pick = b if half == 0 else a
         odd_pick = a if half == 0 else b
-        return given_refs[r][i].astype(F32) + jnp.where(parity == 0, even_pick, odd_pick)
+        return given[position ^ r, i].astype(F32) + jnp.where(parity == 0, even_pick, odd_pick)
 
     return block
 
@@ -136,70 +145,65 @@
     return store
 
 
-def first_sweep_kernel(edge, m0, m1, m2, m3, g0, g1, g2, g3, to_a, to_b, turned, z):
-    parity = lax.axis_index("dom") % 2
-    given = (g0, g1, g2, g3)
+def first_sweep_kernel(edge, m0, m1, m2, m3, given, to_a, to_b, turned, z):
+    position, parity = lax.axis_index("sub") % 4, lax.axis_index("dom") % 2
     for r, m in enumerate((m0, m1, m2, m3)):
         turned[r] = m[...].T
-    chain(
-        edge, turned, lambda r, i: given[r][i].astype(F32), send_store(to_a, to_b, parity), z
-    )
-
-
-def next_sweep_kernel(edge, turned, g0, g1, g2, g3, got_a, got_b, to_a, to_b, v, z):
+    base = lambda r, i: given[position ^ r, i].astype(F32)
+    chain(edge, turned, base, send_store(to_a, to_b, parity), z)
+
+
+def next_sweep_kernel(edge, turned, given, got_a, got_b, to_a, to_b, v, z):
     parity = lax.axis_index("dom") % 2
-    block = swapped_in((g0, g1, g2, g3), got_a, got_b, parity)
+    block = swapped_in(given, got_a, got_b)
     for r in range(4):
         for i in range(4):
             v[r, i] = block(r, i).astype(BF16)
-    chain(
-        edge, turned, lambda r, i: v[r, i].astype(F32), send_store(to_a, to_b, parity), z
-    )
+    base = lambda r, i: v[r, i].astype(F32)
+    chain(edge, turned, base, send_store(to_a, to_b, parity), z)
 
 
 def first_sweep(edge, maps, given):
-    blocks, width, _ = given[0].shape
+    _, blocks, width, _ = given.shape
     sent = pltpu.VMEM((4, blocks // 2, width, EDGE), BF16)
     turned = pltpu.VMEM((4,) + maps[0].shape, BF16)
     z = pltpu.VMEM((2, 4 * blocks, width, EDGE), F32)
-    return call(first_sweep_kernel, (sent, sent, turned), (*maps, *given), (z,), edge)
+    return call(first_sweep_kernel, (sent, sent, turned), (*maps, given), (z,), edge)
 
 
 def next_sweep(edge, turned, given, got):
-    blocks, width, _ = given[0].shape
+    _, blocks, width, _ = given.shape
     sent = pltpu.VMEM((4, blocks // 2, width, EDGE), BF16)
-    v = pltpu.VMEM((4, blocks, width, EDGE), BF16)
+    v = pltpu.VMEM(given.shape, BF16)
     z = pltpu.VMEM((2, 4 * blocks, width, EDGE), F32)
-    return call(next_sweep_kernel, (sent, sent), (turned, *given, *got), (v, z), edge)
-
-
-def join_kernel(g0, g1, g2, g3, got_a, got_b, *out_refs):
-    parity = lax.axis_index("dom") % 2
-    block = swapped_in((g0, g1, g2, g3), got_a, got_b, parity)
+    return call(next_sweep_kernel, (sent, sent), (turned, given, *got), (v, z), edge)
+
+
+def join_kernel(given, got_a, got_b, out):
+    position = lax.axis_index("sub") % 4
+    block = swapped_in(given, got_a, got_b)
     for r in range(4):
         for i in range(4):
-            out_refs[r][i] = block(r, i).astype(BF16)
+            out[position ^ r, i] = block(r, i).astype(BF16)
 
 
 def join(given, got):
-    return call(join_kernel, (pltpu.VMEM(given[0].shape, BF16),) * 4, (*given, *got))
-
-
-def leaf_kernel(own, u0, u1, u2, u3, out, turned):
-    position = lax.axis_index("sub") % 4
-    width = u0.shape[1]
-    for r, u in enumerate((u0, u1, u2, u3)):
-        rows = pl.ds(pl.multiple_of((position ^ r) * width, width), width)
-        for i in range(4):
-            turned[rows, i * EDGE : (i + 1) * EDGE] = u[i]
+    return call(join_kernel, pltpu.VMEM(given.shape, BF16), (given, *got))
+
+
+def leaf_kernel(own, pieces, out, turned):
+    width = pieces.shape[2]
+    for k in range(4):
+        for i in range(4):
+            turned[k * width : (k + 1) * width, i * EDGE : (i + 1) * EDGE] = pieces[k, i]
     out[...] = lax.dot_general(own[...], turned[...], NT, preferred_element_type=F32)
 
 
 def leaf_product(own, pieces):
-    blocks, width, _ = pieces[0].shape
+    _, blocks, width, _ = pieces.shape
     result = jax.ShapeDtypeStruct((own.shape[0], 4 * width), F32)
     turned = pltpu.VMEM((4 * width, blocks * EDGE), BF16)
-    return call(leaf_kernel, result, (own, *pieces), (turned,))
+    return call(leaf_kernel, result, (own, pieces), (turned,))
 
 
 def apply_once(edge_ref, map_refs, source, target):
@@ -230,12 +234,27 @@
 
 def merge(edge, maps, source):
     width = maps[0].shape[0]
-    shape = (4 * width // EDGE, EDGE, width)
-    work = pltpu.VMEM(shape, BF16)
+    work = pltpu.VMEM((4 * width // EDGE, EDGE, width), BF16)
     if source is None:
         return call(merge_first_kernel, work, maps, (work,), edge)
-    result = jax.ShapeDtypeStruct(shape, BF16)
-    return call(merge_next_kernel, result, (*maps, source), (work,), edge)
+    return call(merge_next_kernel, work, (*maps, source), (work,), edge)
+
+
+def store_kernel(value, out, sem):
+    copy = pltpu.make_async_copy(value, out, sem)
+    copy.start()
+    copy.wait()
+
+
+def store(value):
+    return pl.pallas_call(
+        store_kernel,
+        out_shape=jax.ShapeDtypeStruct(value.shape, value.dtype),
+        in_specs=[VMEM],
+        out_specs=pl.BlockSpec(memory_space=pltpu.HBM),
+        scratch_shapes=[pltpu.SemaphoreType.DMA],
+        compiler_params=pltpu.CompilerParams(vmem_limit_bytes=1 << 20),
+    )(value)
 
 
 def per_device(leaf_maps, edge, incoming):
@@ -245,11 +264,9 @@
 def steps(own, edge, incoming):
     width = own.shape[0]
     across = sub_partner(own, 2)
-    edge, own_near, mine = split_rhs(edge, own, near(incoming))
-    given = [mine[0]]
+    edge, own_near, mine = split_rhs(edge, own, incoming)
     beside = sub_partner(own, 1)
-    for r in (1, 2, 3):
-        given.append(sub_partner(mine[r], r))
+    given = group_exchange(mine)
     opposite = sub_partner(across, 1)
     maps = (own_near, beside, across, opposite)
 
@@ -259,14 +276,13 @@
 
     *sent, turned = first_sweep(edge, maps, given)
     got = swap(sent)
-    half_merged = merge(edge, maps, None)
+    merged = merge(edge, maps, None)
     sent = next_sweep(edge, turned, given, got)
     got = swap(sent)
-    merged = merge(edge, maps, half_merged)
+    merged = merge(edge, maps, merged)
     mine = join(given, got)
-    pieces = [mine[0]]
-    for r in (1, 2, 3):
-        pieces.append(sub_partner(mine[r], r))
+    pieces = group_exchange(mine)
+    merged = store(merged)
     leaf_out = leaf_product(own_near, pieces)
     return merged.reshape(1, 1, 4 * width, width), leaf_out[None, None]
 

time: 85.2 us -> 75.9 us (0.89)
  starting transfers between devices: 54.3 us -> 43.3 us
  blocking collectives: 0 us -> 7.66 us
  waiting for transfers between devices: 10.9 us -> 6.79 us
  local copies, waits for them, and re-layouts: 2.73 us -> 0 us
  Pallas kernels: 15.9 us -> 17 us
    ppermute x9 -> x3, starting transfers between devices: 36 us -> 17.9 us  [sub_partner(): lax.ppermute(value, 'sub', [(i, i ^ mask) for i in range(size)])]
    all_to_all x0 -> x1, blocking collectives: none -> 7.66 us  [group_exchange(): return near(lax.all_to_all(value, 'sub', 0, 0, axis_index_groups=groups))]
    all_to_all x0 -> x1, starting transfers between devices: none -> 6.99 us  [group_exchange(): return near(lax.all_to_all(value, 'sub', 0, 0, axis_index_groups=groups))]
    ppermute x9 -> x3, waiting for transfers between devices: 5.73 us -> 2.06 us  [sub_partner(): lax.ppermute(value, 'sub', [(i, i ^ mask) for i in range(size)])]
    unnamed x6 -> x0, local copies, waits for them, and re-layouts: 2.73 us -> none
    pallas_call x0 -> x1, Pallas kernels: none -> 1.33 us  [store(): pl.pallas_call(store_kernel, out_shape=jax.ShapeDtypeStruct(value.shape,...]
  transfers between devices with their start and end apart: 13 -> 8, of which waited for: 4 -> 3; matrix products, arithmetic and copies ran while one was open for 0% -> 0% of each run, Pallas kernels for 9% -> 10%
where the time goes in v1:
time: 75.9 us; the launch traced here: 75.4 us
  starting transfers between devices  43.3 us (57%)
  Pallas kernels  17 us (22%)
  blocking collectives  7.66 us (10%)
  waiting for transfers between devices  6.79 us (9%)
  between operations  0.76 us (1%)
    ppermute x4, starting transfers between devices, dom_partner(): return near(lax.ppermute(value, 'dom', pairs))  18.3 us
    ppermute x3, starting transfers between devices, sub_partner(): lax.ppermute(value, 'sub', [(i, i ^ mask) for i in range(size)])  17.9 us
    pallas_call x6, Pallas kernels, call(): pl.pallas_call(kernel, out_shape=results, in_specs=specs, out_specs=(VMEM...  14.4 us
    all_to_all x1, blocking collectives, group_exchange(): return near(lax.all_to_all(value, 'sub', 0, 0, axis_index_groups=groups))  7.66 us
    all_to_all x1, starting transfers between devices, group_exchange(): return near(lax.all_to_all(value, 'sub', 0, 0, axis_index_groups=groups))  6.99 us
    ppermute x4, waiting for transfers between devices, dom_partner(): return near(lax.ppermute(value, 'dom', pairs))  4.72 us
    ppermute x3, waiting for transfers between devices, sub_partner(): lax.ppermute(value, 'sub', [(i, i ^ mask) for i in range(size)])  2.06 us
  transfers between devices with their start and end apart: 8, of which 3 were waited for; matrix products, arithmetic and copies ran while one was open for 0% of the time, Pallas kernels for 10%

profile of v1, /device:TPU:1, one launch (start us, length us, event | category | flops | bytes accessed | tf_op | source)
XLA Modules:
  0.0 75.4 jit_solution(10772591370437625063)
XLA Ops:
  0.6 4.8 %collective-permute-start.1 = (bf16[512,512]{1,0:T(8,128)(2,1)}, bf16[512,512]{1,0:T(8,128)(2,1)S(1)}, u32[]{:S(2)}, u32[]{:S(2)}) collective-permute-start(bf16[512,512]{1,0:T(8,128)(2,1)} %bitcast.7), channel_id=1, source_target_pairs={{0,64},{32,96},{64,0},{96,32},{128,192},{160,224},{192,128},{224,1... | collective-permute-start | bytes 1572872 | tf_op jit(solution)/shard_map/ppermute | solution.py:44
  5.5 5.8 %collective-permute-start = (bf16[512,512]{1,0:T(8,128)(2,1)}, bf16[512,512]{1,0:T(8,128)(2,1)S(1)}, u32[]{:S(2)}, u32[]{:S(2)}) collective-permute-start(bf16[512,512]{1,0:T(8,128)(2,1)} %bitcast.8), channel_id=1, source_target_pairs={{0,32},{32,0},{64,96},{96,64},{128,160},{160,128},{192,224},{224,1... | collective-permute-start | bytes 1572872 | tf_op jit(solution)/shard_map/ppermute | solution.py:44
  11.3 2.1 %collective-permute-done.1.m2 = bf16[512,512]{1,0:T(8,128)(2,1)S(1)} collective-permute-done((bf16[512,512]{1,0:T(8,128)(2,1)}, bf16[512,512]{1,0:T(8,128)(2,1)S(1)}, u32[]{:S(2)}, u32[]{:S(2)}) %collective-permute-start.1) | collective-permute-done | bytes 524320 | tf_op jit(solution)/shard_map/ppermute | solution.py:44
  13.4 7.3 %collective-permute-start.2 = (bf16[512,512]{1,0:T(8,128)(2,1)S(1)}, bf16[512,512]{1,0:T(8,128)(2,1)S(1)}, u32[]{:S(2)}, u32[]{:S(2)}) collective-permute-start(bf16[512,512]{1,0:T(8,128)(2,1)S(1)} %collective-permute-done.1.m2), channel_id=1, source_target_pairs={{0,32},{32,0},{64,96},{96,64},{128,160},{160,128},{192,224},{224,1... | collective-permute-start | bytes 1572872 | tf_op jit(solution)/shard_map/ppermute | solution.py:44
  20.7 1.2 %shard_map.50 = (s32[1,16]{1,0:T(1,128)S(4)}, bf16[512,512]{1,0:T(8,128)(2,1)S(1)}, bf16[4,4,64,128]{3,2,1,0:T(8,128)(2,1)S(1)}) custom-call(s32[1,16]{1,0:T(1,128)} %edge_in.1, bf16[512,512]{1,0:T(8,128)(2,1)} %bitcast.9, f32[512,256]{1,0:T(8,128)} %bitcast.6), custom_call_target="tpu_custom_call" | custom-call | tf_op jit(solution)/shard_map/pallas_call | solution.py:82
  21.9 7.7 %all_to_all.10.given = bf16[4,4,64,128]{3,2,1,0:T(8,128)(2,1)S(1)} all-to-all(bf16[4,4,64,128]{3,2,1,0:T(8,128)(2,1)S(1)} %get-tuple-element.12), channel_id=1, replica_groups={{0,32,64,96},{128,160,192,224},{256,288,320,352},{384,416,448,480},{1,3..., dimensions={0} | all-to-all | bytes 524288 | tf_op jit(solution)/shard_map/all_to_all | solution.py:59
  29.6 0.0 collective-permute-done.m1
  29.6 0.0 collective-permute-done.2.m3
  29.6 3.8 %shard_map.54 = (bf16[4,2,64,128]{3,2,1,0:T(8,128)(2,1)S(1)}, bf16[4,2,64,128]{3,2,1,0:T(8,128)(2,1)S(1)}, bf16[4,512,512]{2,1,0:T(8,128)(2,1)S(1)}) custom-call(s32[1,16]{1,0:T(1,128)S(4)} %get-tuple-element.10.edge, bf16[512,512]{1,0:T(8,128)(2,1)S(1)} %get-tuple-element.11.m0.own, bf16[512,512]{1,0:T(8,128)(2,1)S(1)} %collective-permute-done.m1, ...), custom_call_target="tpu_custom_call" | custom-call | tf_op jit(solution)/shard_map/pallas_call | solution.py:29
  33.3 3.1 %collective-permute-start.3 = (bf16[4,2,64,128]{3,2,1,0:T(8,128)(2,1)S(1)}, bf16[4,2,64,128]{3,2,1,0:T(8,128)(2,1)S(1)}, u32[]{:S(2)}, u32[]{:S(2)}) collective-permute-start(bf16[4,2,64,128]{3,2,1,0:T(8,128)(2,1)S(1)} %get-tuple-element.14), channel_id=1, source_target_pairs={{0,1},{1,0},{2,3},{3,2},{4,5},{5,4},{6,7},{7,6},{8,9},{9,8},{10,11... | collective-permute-start | bytes 393224 | tf_op jit(solution)/shard_map/ppermute | solution.py:53
  36.4 6.7 %collective-permute-start.4 = (bf16[4,2,64,128]{3,2,1,0:T(8,128)(2,1)S(1)}, bf16[4,2,64,128]{3,2,1,0:T(8,128)(2,1)S(1)}, u32[]{:S(2)}, u32[]{:S(2)}) collective-permute-start(bf16[4,2,64,128]{3,2,1,0:T(8,128)(2,1)S(1)} %get-tuple-element.15), channel_id=1, source_target_pairs={{1,2},{2,1},{3,4},{4,3},{5,6},{6,5},{7,8},{8,7},{9,10},{10,9},{11,... | collective-permute-start | bytes 393224 | tf_op jit(solution)/shard_map/ppermute | solution.py:53
  43.1 0.0 collective-permute-done.3.got_a
  43.1 2.3 %collective-permute-done.4.got_b = bf16[4,2,64,128]{3,2,1,0:T(8,128)(2,1)S(1)} collective-permute-done((bf16[4,2,64,128]{3,2,1,0:T(8,128)(2,1)S(1)}, bf16[4,2,64,128]{3,2,1,0:T(8,128)(2,1)S(1)}, u32[]{:S(2)}, u32[]{:S(2)}) %collective-permute-start.4) | collective-permute-done | bytes 131104 | tf_op jit(solution)/shard_map/ppermute | solution.py:53
  45.5 3.5 %shard_map.55 = (bf16[4,2,64,128]{3,2,1,0:T(8,128)(2,1)S(1)}, bf16[4,2,64,128]{3,2,1,0:T(8,128)(2,1)S(1)}) custom-call(s32[1,16]{1,0:T(1,128)S(4)} %get-tuple-element.10.edge, bf16[4,512,512]{2,1,0:T(8,128)(2,1)S(1)} %get-tuple-element.13.turned, bf16[4,4,64,128]{3,2,1,0:T(8,128)(2,1)S(1)} %all_to_all.10.given, ...), custom_call_target="tpu_custom_call" | custom-call | tf_op jit(solution)/shard_map/pallas_call | solution.py:29
  49.0 1.9 %collective-permute-start.5 = (bf16[4,2,64,128]{3,2,1,0:T(8,128)(2,1)S(1)}, bf16[4,2,64,128]{3,2,1,0:T(8,128)(2,1)S(1)}, u32[]{:S(2)}, u32[]{:S(2)}) collective-permute-start(bf16[4,2,64,128]{3,2,1,0:T(8,128)(2,1)S(1)} %get-tuple-element.16), channel_id=1, source_target_pairs={{0,1},{1,0},{2,3},{3,2},{4,5},{5,4},{6,7},{7,6},{8,9},{9,8},{10,11... | collective-permute-start | bytes 393224 | tf_op jit(solution)/shard_map/ppermute | solution.py:53
  50.9 6.6 %collective-permute-start.6 = (bf16[4,2,64,128]{3,2,1,0:T(8,128)(2,1)S(1)}, bf16[4,2,64,128]{3,2,1,0:T(8,128)(2,1)S(1)}, u32[]{:S(2)}, u32[]{:S(2)}) collective-permute-start(bf16[4,2,64,128]{3,2,1,0:T(8,128)(2,1)S(1)} %get-tuple-element.17), channel_id=1, source_target_pairs={{1,2},{2,1},{3,4},{4,3},{5,6},{6,5},{7,8},{8,7},{9,10},{10,9},{11,... | collective-permute-start | bytes 393224 | tf_op jit(solution)/shard_map/ppermute | solution.py:53
  57.5 0.0 collective-permute-done.5.got_a
  57.5 2.4 %collective-permute-done.6.got_b = bf16[4,2,64,128]{3,2,1,0:T(8,128)(2,1)S(1)} collective-permute-done((bf16[4,2,64,128]{3,2,1,0:T(8,128)(2,1)S(1)}, bf16[4,2,64,128]{3,2,1,0:T(8,128)(2,1)S(1)}, u32[]{:S(2)}, u32[]{:S(2)}) %collective-permute-start.6) | collective-permute-done | bytes 131104 | tf_op jit(solution)/shard_map/ppermute | solution.py:53
  59.9 0.8 %shard_map.56 = bf16[4,4,64,128]{3,2,1,0:T(8,128)(2,1)} custom-call(bf16[4,4,64,128]{3,2,1,0:T(8,128)(2,1)S(1)} %all_to_all.10.given, bf16[4,2,64,128]{3,2,1,0:T(8,128)(2,1)S(1)} %collective-permute-done.5.got_a, bf16[4,2,64,128]{3,2,1,0:T(8,128)(2,1)S(1)} %collective-permute-done.6.got_b), custom_call_target="tpu_custom_call" | custom-call | tf_op jit(solution)/shard_map/pallas_call | solution.py:29
  60.7 7.0 %all-to-all-start.1 = ((bf16[4,4,64,128]{3,2,1,0:T(8,128)(2,1)}), bf16[4,4,64,128]{3,2,1,0:T(8,128)(2,1)S(1)}, u32[]{:S(2)}, u32[]{:S(2)}) async-start(bf16[4,4,64,128]{3,2,1,0:T(8,128)(2,1)} %shard_map.56), calls=%async_computation.1 | async-start | bytes 524288 | tf_op jit(solution)/shard_map/all_to_all | solution.py:59
  67.7 2.7 %shard_map.51.source = bf16[16,128,512]{2,1,0:T(8,128)(2,1)S(1)} custom-call(s32[1,16]{1,0:T(1,128)S(4)} %get-tuple-element.10.edge, bf16[512,512]{1,0:T(8,128)(2,1)S(1)} %get-tuple-element.11.m0.own, bf16[512,512]{1,0:T(8,128)(2,1)S(1)} %collective-permute-done.m1, bf16[512,512]{1,0:T(8,128)(2,1)S(1)} %collective-permute-done.1.m2, ...), custom_call_target="tpu_custom_call" | custom-call | tf_op jit(solution)/shard_map/pallas_call | solution.py:29
  70.4 2.5 %shard_map.52.value = bf16[16,128,512]{2,1,0:T(8,128)(2,1)S(1)} custom-call(s32[1,16]{1,0:T(1,128)S(4)} %get-tuple-element.10.edge, bf16[512,512]{1,0:T(8,128)(2,1)S(1)} %get-tuple-element.11.m0.own, bf16[512,512]{1,0:T(8,128)(2,1)S(1)} %collective-permute-done.m1, bf16[512,512]{1,0:T(8,128)(2,1)S(1)} %collective-permute-done.1.m2, ...), custom_call_target="tpu_custom_call" | custom-call | tf_op jit(solution)/shard_map/pallas_call | solution.py:29
  73.0 1.3 %shard_map.53 = bf16[16,128,512]{2,1,0:T(8,128)(2,1)} custom-call(bf16[16,128,512]{2,1,0:T(8,128)(2,1)S(1)} %shard_map.52.value), custom_call_target="tpu_custom_call" | custom-call | tf_op jit(solution)/shard_map/pallas_call | solution.py:250
  74.3 0.0 all-to-all-done.1.pieces
  74.3 1.1 %shard_map.57 = f32[512,256]{1,0:T(8,128)} custom-call(bf16[512,512]{1,0:T(8,128)(2,1)S(1)} %get-tuple-element.11.m0.own, bf16[4,4,64,128]{3,2,1,0:T(8,128)(2,1)S(1)} %all-to-all-done.1.pieces), custom_call_target="tpu_custom_call" | custom-call | tf_op jit(solution)/shard_map/pallas_call | solution.py:29
Async XLA Ops:
  0.6 12.7 %collective-permute-start.1 = (bf16[512,512]{1,0:T(8,128)(2,1)}, bf16[512,512]{1,0:T(8,128)(2,1)S(1)}, u32[]{:S(2)}, u32[]{:S(2)}) collective-permute-start(bf16[512,512]{1,0:T(8,128)(2,1)} %bitcast.7), channel_id=1, source_target_pairs={{0,64},{32,96},{64,0},{96,32},{128,192},{160,224},{192,128},{224,1... | collective-permute-start | bytes 1572872 | tf_op jit(solution)/shard_map/ppermute | solution.py:44
  5.5 24.1 %collective-permute-start = (bf16[512,512]{1,0:T(8,128)(2,1)}, bf16[512,512]{1,0:T(8,128)(2,1)S(1)}, u32[]{:S(2)}, u32[]{:S(2)}) collective-permute-start(bf16[512,512]{1,0:T(8,128)(2,1)} %bitcast.8), channel_id=1, source_target_pairs={{0,32},{32,0},{64,96},{96,64},{128,160},{160,128},{192,224},{224,1... | collective-permute-start | bytes 1572872 | tf_op jit(solution)/shard_map/ppermute | solution.py:44
  13.4 16.2 %collective-permute-start.2 = (bf16[512,512]{1,0:T(8,128)(2,1)S(1)}, bf16[512,512]{1,0:T(8,128)(2,1)S(1)}, u32[]{:S(2)}, u32[]{:S(2)}) collective-permute-start(bf16[512,512]{1,0:T(8,128)(2,1)S(1)} %collective-permute-done.1.m2), channel_id=1, source_target_pairs={{0,32},{32,0},{64,96},{96,64},{128,160},{160,128},{192,224},{224,1... | collective-permute-start | bytes 1572872 | tf_op jit(solution)/shard_map/ppermute | solution.py:44
  33.3 9.8 %collective-permute-start.3 = (bf16[4,2,64,128]{3,2,1,0:T(8,128)(2,1)S(1)}, bf16[4,2,64,128]{3,2,1,0:T(8,128)(2,1)S(1)}, u32[]{:S(2)}, u32[]{:S(2)}) collective-permute-start(bf16[4,2,64,128]{3,2,1,0:T(8,128)(2,1)S(1)} %get-tuple-element.14), channel_id=1, source_target_pairs={{0,1},{1,0},{2,3},{3,2},{4,5},{5,4},{6,7},{7,6},{8,9},{9,8},{10,11... | collective-permute-start | bytes 393224 | tf_op jit(solution)/shard_map/ppermute | solution.py:53
  36.4 9.0 %collective-permute-start.4 = (bf16[4,2,64,128]{3,2,1,0:T(8,128)(2,1)S(1)}, bf16[4,2,64,128]{3,2,1,0:T(8,128)(2,1)S(1)}, u32[]{:S(2)}, u32[]{:S(2)}) collective-permute-start(bf16[4,2,64,128]{3,2,1,0:T(8,128)(2,1)S(1)} %get-tuple-element.15), channel_id=1, source_target_pairs={{1,2},{2,1},{3,4},{4,3},{5,6},{6,5},{7,8},{8,7},{9,10},{10,9},{11,... | collective-permute-start | bytes 393224 | tf_op jit(solution)/shard_map/ppermute | solution.py:53
  49.0 8.6 %collective-permute-start.5 = (bf16[4,2,64,128]{3,2,1,0:T(8,128)(2,1)S(1)}, bf16[4,2,64,128]{3,2,1,0:T(8,128)(2,1)S(1)}, u32[]{:S(2)}, u32[]{:S(2)}) collective-permute-start(bf16[4,2,64,128]{3,2,1,0:T(8,128)(2,1)S(1)} %get-tuple-element.16), channel_id=1, source_target_pairs={{0,1},{1,0},{2,3},{3,2},{4,5},{5,4},{6,7},{7,6},{8,9},{9,8},{10,11... | collective-permute-start | bytes 393224 | tf_op jit(solution)/shard_map/ppermute | solution.py:53
  50.9 9.0 %collective-permute-start.6 = (bf16[4,2,64,128]{3,2,1,0:T(8,128)(2,1)S(1)}, bf16[4,2,64,128]{3,2,1,0:T(8,128)(2,1)S(1)}, u32[]{:S(2)}, u32[]{:S(2)}) collective-permute-start(bf16[4,2,64,128]{3,2,1,0:T(8,128)(2,1)S(1)} %get-tuple-element.17), channel_id=1, source_target_pairs={{1,2},{2,1},{3,4},{4,3},{5,6},{6,5},{7,8},{8,7},{9,10},{10,9},{11,... | collective-permute-start | bytes 393224 | tf_op jit(solution)/shard_map/ppermute | solution.py:53
  60.7 13.6 %all-to-all-start.1 = ((bf16[4,4,64,128]{3,2,1,0:T(8,128)(2,1)}), bf16[4,4,64,128]{3,2,1,0:T(8,128)(2,1)S(1)}, u32[]{:S(2)}, u32[]{:S(2)}) async-start(bf16[4,4,64,128]{3,2,1,0:T(8,128)(2,1)} %shard_map.56), calls=%async_computation.1 | async-start | bytes 524288 | tf_op jit(solution)/shard_map/all_to_all | solution.py:59

commit v2 on v1

v2 whole, which is shorter than its diff:
```python
import jax
import jax.numpy as jnp
from jax import lax
from jax.experimental import pallas as pl
from jax.experimental.pallas import tpu as pltpu
from jax.sharding import PartitionSpec as P


KTERMS = 4
EDGE = 128
NT = (((1,), (1,)), ((), ()))
BF16 = jnp.bfloat16
F32 = jnp.float32
VMEM = pl.BlockSpec(memory_space=pltpu.VMEM)
EMPTY = pltpu.VMEM((8, 128), F32)
SMEM = pl.BlockSpec(memory_space=pltpu.SMEM)


def near(value):
    return pltpu.with_memory_space_constraint(value, pltpu.VMEM)


def call(kernel, results, args, scratch=(), edge=None):
    specs = [VMEM] * len(args)
    args = list(args)
    if edge is not None:
        specs, args = [SMEM] + specs, [edge] + args
    many = isinstance(results, tuple)
    made = pl.pallas_call(
        kernel,
        out_shape=results,
        in_specs=specs,
        out_specs=(VMEM,) * len(results) if many else VMEM,
        scratch_shapes=list(scratch),
        compiler_params=pltpu.CompilerParams(vmem_limit_bytes=16 << 20),
    )(*args)
    if many:
        return tuple(near(m) for m in made)
    return near(made) if isinstance(results, type(EMPTY)) else made


def sub_partner(value, mask):
    size = lax.axis_size("sub")
    return near(lax.ppermute(value, "sub", [(i, i ^ mask) for i in range(size)]))


def dom_pairs(first):
    size = lax.axis_size("dom")
    pairs = []
    for low in range(first, first + size, 2):
        left, right = low % size, (low + 1) % size
        pairs += [(left, right), (right, left)]
    return pairs


def dom_partner(value, first):
    return near(lax.ppermute(value, "dom", dom_pairs(first)))


def cross_partner(value, first, mask):
    size = lax.axis_size("dom")
    pairs = [
        (s * size + a, (s ^ mask) * size + b)
        for s in range(lax.axis_size("sub"))
        for a, b in dom_pairs(first)
    ]
    return near(lax.ppermute(value, ("sub", "dom"), pairs))


def group_exchange(value):
    size = lax.axis_size("sub")
    groups = [list(range(g, g + 4)) for g in range(0, size, 4)]
    return near(lax.all_to_all(value, "sub", 0, 0, axis_index_groups=groups))


def split_kernel(edge_in, own_in, x_in, edge_out, own_out, pieces, kept, x_ref, sems):
    fetch = pltpu.make_async_copy(x_in, x_ref, sems.at[0])
    others = [
        pltpu.make_async_copy(edge_in, edge_out, sems.at[1]),
        pltpu.make_async_copy(own_in, own_out, sems.at[2]),
    ]
    for copy in [fetch] + others:
        copy.start()
    fetch.wait()
    turned = x_ref[...].T.astype(BF16)
    width = turned.shape[0] // 4
    for k in range(4):
        for i in range(4):
            block = turned[k * width : (k + 1) * width, i * EDGE : (i + 1) * EDGE]
            pieces[k, i] = block
            kept[k, i] = block
    for copy in others:
        copy.wait()


def split_rhs(edge, own, x):
    rows, cols = x.shape
    piece = pltpu.VMEM((4, rows // EDGE, cols // 4, EDGE), BF16)
    edge, own, pieces, kept = pl.pallas_call(
        split_kernel,
        out_shape=(
            pltpu.SMEM(edge.shape, jnp.int32),
            pltpu.VMEM(own.shape, BF16),
            piece,
            piece,
        ),
        in_specs=[pl.BlockSpec(memory_space=pltpu.HBM)] * 3,
        out_specs=(SMEM, VMEM, VMEM, VMEM),
        scratch_shapes=[pltpu.VMEM(x.shape, F32), pltpu.SemaphoreType.DMA((3,))],
        compiler_params=pltpu.CompilerParams(vmem_limit_bytes=16 << 20),
    )(*(pltpu.with_memory_space_constraint(a, pltpu.HBM) for a in (edge, own, x)))
    edge = pltpu.with_memory_space_constraint(edge, pltpu.SMEM)
    return edge, near(own), near(pieces), near(kept)


def swapped_in(given, got_a, got_b):
    position, parity = lax.axis_index("sub") % 4, lax.axis_index("dom") % 2

    def block(r, i):
        half, k = i // 2, i % 2
        a, b = got_a[r, k].astype(F32), got_b[r, k].astype(F32)
        even_pick = b if half == 0 else a
        odd_pick = a if half == 0 else b
        return given[position ^ r, i].astype(F32) + jnp.where(parity == 0, even_pick, odd_pick)

    return block


def chain(edge_ref, turned_pairs, base_block, store, z_ref):
    position = lax.axis_index("sub") % 4
    for step in range(KTERMS + 1):
        slot, before = step % 2, (step + 1) % 2
        for r in range(4):
            leaf = position ^ r
            parts = []
            for i in range(4):
                part = base_block(r, i)
                if step > 0:
                    part = part + z_ref[before, edge_ref[0, leaf * 4 + i]]
                parts.append(part.astype(BF16))
            operand = jnp.concatenate(parts, 1)
            turned = turned_pairs[r // 2][r % 2]
            out = jnp.dot(operand, turned, preferred_element_type=F32)
            for i in range(4):
                value = out[:, i * EDGE : (i + 1) * EDGE]
                if step == KTERMS:
                    store(r, i, value)
                else:
                    z_ref[slot, leaf * 4 + i] = value


def send_store(to_near, to_far, parity):
    def store(r, i, value):
        half, k = i // 2, i % 2
        value = value.astype(BF16)
        run = 4 // len(to_near)

        @pl.when(parity == half)
        def _():
            to_far[r // run][r % run, k] = value

        @pl.when(parity != half)
        def _():
            to_near[r // run][r % run, k] = value

    return store


def first_sweep_kernel(edge, here, m2, m3, given, to_a, to_b, come, z):
    position, parity = lax.axis_index("sub") % 4, lax.axis_index("dom") % 2
    for k, m in enumerate((m2, m3)):
        come[k] = m[...].T
    base = lambda r, i: given[position ^ r, i].astype(F32)
    chain(edge, (here, come), base, send_store((to_a,), (to_b,), parity), z)


def next_sweep_kernel(edge, here, come, given, got_a, got_b, n0, n2, f0, f2, v, z):
    parity = lax.axis_index("dom") % 2
    block = swapped_in(given, got_a, got_b)
    for r in range(4):
        for i in range(4):
            v[r, i] = block(r, i).astype(BF16)
    base = lambda r, i: v[r, i].astype(F32)
    chain(edge, (here, come), base, send_store((n0, n2), (f0, f2), parity), z)


def first_sweep(edge, here, m2, m3, given):
    _, blocks, width, _ = given.shape
    sent = pltpu.VMEM((4, blocks // 2, width, EDGE), BF16)
    come = pltpu.VMEM(here.shape, BF16)
    z = pltpu.VMEM((2, 4 * blocks, width, EDGE), F32)
    return call(first_sweep_kernel, (sent, sent, come), (here, m2, m3, given), (z,), edge)


def next_sweep(edge, here, come, given, got):
    _, blocks, width, _ = given.shape
    sent = pltpu.VMEM((2, blocks // 2, width, EDGE), BF16)
    v = pltpu.VMEM(given.shape, BF16)
    z = pltpu.VMEM((2, 4 * blocks, width, EDGE), F32)
    return call(next_sweep_kernel, (sent,) * 4, (here, come, given, *got), (v, z), edge)


def picked(near_ref, far_ref, leaf, i, parity):
    half, k = i // 2, i % 2
    return jnp.where(parity == half, far_ref[leaf, k].astype(F32), near_ref[leaf, k].astype(F32))


def join_kernel(n0, n2, f0, f2, out):
    parity = lax.axis_index("dom") % 2
    for k, refs in enumerate(((n0, f0), (n2, f2))):
        for i in range(4):
            out[k, i] = picked(*refs, 1, i, parity).astype(BF16)


def join(got):
    _, halves, width, _ = got[0].shape
    return call(join_kernel, pltpu.VMEM((2, 2 * halves, width, EDGE), BF16), got)


def leaf_kernel(own, kept, n0, n2, f0, f2, others, out, turned):
    position, parity = lax.axis_index("sub") % 4, lax.axis_index("dom") % 2
    width = kept.shape[2]
    for r in range(4):
        member = position ^ r
        rows = pl.ds(pl.multiple_of(member * width, width), width)
        for i in range(4):
            if r % 2 == 0:
                refs = (n0, f0) if r == 0 else (n2, f2)
                value = picked(*refs, 0, i, parity)
            else:
                value = others[r // 2, i].astype(F32)
            u = kept[member, i].astype(F32) + value
            turned[rows, i * EDGE : (i + 1) * EDGE] = u.astype(BF16)
    out[...] = lax.dot_general(own[...], turned[...], NT, preferred_element_type=F32)


def leaf_product(own, kept, got, others):
    _, blocks, width, _ = kept.shape
    result = jax.ShapeDtypeStruct((own.shape[0], 4 * width), F32)
    turned = pltpu.VMEM((4 * width, blocks * EDGE), BF16)
    return call(leaf_kernel, result, (own, kept, *got, others), (turned,))


def apply_once(edge_ref, map_refs, source, target, leaves=range(4)):
    position = lax.axis_index("sub") % 4
    for r in leaves:
        leaf = position ^ r
        operand = jnp.concatenate([source[edge_ref[0, leaf * 4 + i]] for i in range(4)], 0)
        out = jnp.dot(map_refs[r][...], operand, preferred_element_type=F32)
        if r == 0:
            out = out + map_refs[0][...].astype(F32)
        for i in range(4):
            target[leaf * 4 + i] = out[i * EDGE : (i + 1) * EDGE].astype(BF16)


def apply_first(edge_ref, m_ref, own_ref, r):
    position = lax.axis_index("sub") % 4
    parts = []
    for i in range(4):
        block = edge_ref[0, (position ^ r) * 4 + i]
        rows = own_ref[pl.ds(pl.multiple_of(block % 4 * EDGE, EDGE), EDGE), :]
        parts.append(jnp.where(block // 4 == position, rows, jnp.zeros_like(rows)))
    out = jnp.dot(m_ref[...], jnp.concatenate(parts, 0), preferred_element_type=F32)
    if r == 0:
        out = out + own_ref[...].astype(F32)
    return [out[i * EDGE : (i + 1) * EDGE].astype(BF16) for i in range(4)]


def early_kernel(edge, m0, m1, here, begun):
    for r, m in enumerate((m0, m1)):
        here[r] = m[...].T
        for i, value in enumerate(apply_first(edge, m, m0, r)):
            begun[r, i] = value


def early(edge, own, beside):
    here = pltpu.VMEM((2,) + own.shape, BF16)
    begun = pltpu.VMEM((2, 4, EDGE, own.shape[1]), BF16)
    return call(early_kernel, (here, begun), (own, beside), (), edge)


def merge_first_kernel(edge, m0, m1, m2, m3, begun, out, work):
    position = lax.axis_index("sub") % 4
    for r in range(2):
        for i in range(4):
            work[(position ^ r) * 4 + i] = begun[r, i]
    for r, m in ((2, m2), (3, m3)):
        for i, value in enumerate(apply_first(edge, m, m0, r)):
            work[(position ^ r) * 4 + i] = value
    apply_once(edge, (m0, m1, m2, m3), work, out)


def merge_next_kernel(edge, m0, m1, m2, m3, source, out, work, last, sems):
    maps = (m0, m1, m2, m3)
    position = lax.axis_index("sub") % 4
    apply_once(edge, maps, source, work)
    copies = []
    for r in range(4):
        apply_once(edge, maps, work, last, (r,))
        blocks = pl.ds((position ^ r) * 4, 4)
        copies.append(pltpu.make_async_copy(last.at[blocks], out.at[blocks], sems.at[r]))
        copies[-1].start()
    for copy in copies:
        copy.wait()


def merge_first(edge, maps, begun):
    width = maps[0].shape[0]
    work = pltpu.VMEM((4 * width // EDGE, EDGE, width), BF16)
    return call(merge_first_kernel, work, (*maps, begun), (work,), edge)


def merge_last(edge, maps, source):
    return pl.pallas_call(
        merge_next_kernel,
        out_shape=jax.ShapeDtypeStruct(source.shape, BF16),
        in_specs=[SMEM] + [VMEM] * 5,
        out_specs=pl.BlockSpec(memory_space=pltpu.HBM),
        scratch_shapes=[pltpu.VMEM(source.shape, BF16)] * 2 + [pltpu.SemaphoreType.DMA((4,))],
        compiler_params=pltpu.CompilerParams(vmem_limit_bytes=16 << 20),
    )(edge, *maps, source)


def per_device(leaf_maps, edge, incoming):
    return steps(leaf_maps[0, 0], edge, incoming[0, 0])


def steps(own, edge, incoming):
    width = own.shape[0]
    across = sub_partner(own, 2)
    edge, own_near, mine, kept = split_rhs(edge, own, incoming)
    beside = sub_partner(own, 1)
    here, begun = early(edge, own_near, beside)
    given = group_exchange(mine)
    opposite = sub_partner(across, 1)
    maps = (own_near, beside, across, opposite)

    def swap(sent):
        far = dom_partner(sent[1], 1)
        return dom_partner(sent[0], 0), far

    *sent, come = first_sweep(edge, here, across, opposite, given)
    got = swap(sent)
    merged = merge_first(edge, maps, begun)
    sent = next_sweep(edge, here, come, given, got)
    far2 = cross_partner(sent[3], 1, 2)
    far0 = dom_partner(sent[2], 1)
    near2 = cross_partner(sent[1], 0, 2)
    near0 = dom_partner(sent[0], 0)
    got = (near0, near2, far0, far2)
    merged = merge_last(edge, maps, merged)
    mine = join(got)
    others = sub_partner(mine, 1)
    leaf_out = leaf_product(own_near, kept, got, others)
    return merged.reshape(1, 1, 4 * width, width), leaf_out[None, None]


def solution(mesh):
    placed = (P("dom", "sub", None, None), P("dom", None), P("dom", "sub", None, None))
    return jax.shard_map(
        per_device,
        mesh=mesh,
        in_specs=placed,
        out_specs=(P("dom", "sub", None, None), P("dom", "sub", None, None)),
        check_vma=False,
    )
```

time: 75.9 us -> 85.4 us (1.13)
  starting transfers between devices: 43.3 us -> 51.6 us
  blocking collectives: 7.66 us -> 0 us
  waiting for transfers between devices: 6.79 us -> 14.4 us
  local copies, waits for them, and re-layouts: 0 us -> 1.66 us
    all_to_all x1 -> x0, blocking collectives: 7.66 us -> none  [group_exchange(): return near(lax.all_to_all(value, 'sub', 0, 0, axis_index_groups=groups))]
    ppermute x4 -> x6, starting transfers between devices: 18.3 us -> 24.6 us  [the longest x4 18.4 us: dom_partner(): return near(lax.ppermute(value, 'dom', dom_pairs(first)))]
    ppermute x3 -> x4, starting transfers between devices: 17.9 us -> 23.6 us  [sub_partner(): lax.ppermute(value, 'sub', [(i, i ^ mask) for i in range(size)])]
    ppermute x4 -> x6, waiting for transfers between devices: 4.72 us -> 9.05 us  [the longest x2 6.69 us: cross_partner(): return near(lax.ppermute(value, ('sub', 'dom'), pairs))]
    all_to_all x1, starting transfers between devices: 6.99 us -> 3.4 us  [group_exchange(): return near(lax.all_to_all(value, 'sub', 0, 0, axis_index_groups=groups))]
    all_to_all x1, waiting for transfers between devices: 0.01 us -> 3.28 us  [group_exchange(): return near(lax.all_to_all(value, 'sub', 0, 0, axis_index_groups=groups))]
    pallas_call x6, Pallas kernels: 14.4 us -> 11.1 us  [call(): pl.pallas_call(kernel, out_shape=results, in_specs=specs, out_specs=(VMEM...]
    pallas_call x1, Pallas kernels: 1.33 us -> 3.36 us  [merge_last(): pl.pallas_call(merge_next_kernel, out_shape=jax.ShapeDtypeStruct(source.s...]
  transfers between devices with their start and end apart: 8 -> 11, of which waited for: 3 -> 4; matrix products, arithmetic and copies ran while one was open for 0% -> 0% of each run, Pallas kernels for 10% -> 10%
where the time goes in v2:
time: 85.4 us; the launch traced here: 85 us
  starting transfers between devices  51.6 us (60%)
  Pallas kernels  16.4 us (19%)
  waiting for transfers between devices  14.4 us (17%)
  local copies, waits for them, and re-layouts  1.66 us (2%)
  between operations  0.87 us (1%)
    ppermute x4, starting transfers between devices, sub_partner(): lax.ppermute(value, 'sub', [(i, i ^ mask) for i in range(size)])  23.6 us
    ppermute x4, starting transfers between devices, dom_partner(): return near(lax.ppermute(value, 'dom', dom_pairs(first)))  18.4 us
    pallas_call x6, Pallas kernels, call(): pl.pallas_call(kernel, out_shape=results, in_specs=specs, out_specs=(VMEM...  11.1 us
    ppermute x2, waiting for transfers between devices, cross_partner(): return near(lax.ppermute(value, ('sub', 'dom'), pairs))  6.69 us
    ppermute x2, starting transfers between devices, cross_partner(): return near(lax.ppermute(value, ('sub', 'dom'), pairs))  6.24 us
    all_to_all x1, starting transfers between devices, group_exchange(): return near(lax.all_to_all(value, 'sub', 0, 0, axis_index_groups=groups))  3.4 us
    pallas_call x1, Pallas kernels, merge_last(): pl.pallas_call(merge_next_kernel, out_shape=jax.ShapeDtypeStruct(source.s...  3.36 us
    all_to_all x1, waiting for transfers between devices, group_exchange(): return near(lax.all_to_all(value, 'sub', 0, 0, axis_index_groups=groups))  3.28 us
  transfers between devices with their start and end apart: 11, of which 4 were waited for; matrix products, arithmetic and copies ran while one was open for 0% of the time, Pallas kernels for 10%

profile of v2, /device:TPU:1, one launch (start us, length us, event | category | flops | bytes accessed | tf_op | source)
XLA Modules:
  0.0 85.0 jit_solution(14816768020025260011)
XLA Ops:
  0.6 4.8 %collective-permute-start.1 = (bf16[512,512]{1,0:T(8,128)(2,1)}, bf16[512,512]{1,0:T(8,128)(2,1)S(1)}, u32[]{:S(2)}, u32[]{:S(2)}) collective-permute-start(bf16[512,512]{1,0:T(8,128)(2,1)} %bitcast.7), channel_id=1, source_target_pairs={{0,64},{32,96},{64,0},{96,32},{128,192},{160,224},{192,128},{224,1... | collective-permute-start | bytes 1572872 | tf_op jit(solution)/shard_map/ppermute | solution.py:44
  5.5 5.8 %collective-permute-start = (bf16[512,512]{1,0:T(8,128)(2,1)}, bf16[512,512]{1,0:T(8,128)(2,1)S(1)}, u32[]{:S(2)}, u32[]{:S(2)}) collective-permute-start(bf16[512,512]{1,0:T(8,128)(2,1)} %bitcast.8), channel_id=1, source_target_pairs={{0,32},{32,0},{64,96},{96,64},{128,160},{160,128},{192,224},{224,1... | collective-permute-start | bytes 1572872 | tf_op jit(solution)/shard_map/ppermute | solution.py:44
  11.3 2.1 %collective-permute-done.1.m2 = bf16[512,512]{1,0:T(8,128)(2,1)S(1)} collective-permute-done((bf16[512,512]{1,0:T(8,128)(2,1)}, bf16[512,512]{1,0:T(8,128)(2,1)S(1)}, u32[]{:S(2)}, u32[]{:S(2)}) %collective-permute-start.1) | collective-permute-done | bytes 524320 | tf_op jit(solution)/shard_map/ppermute | solution.py:44
  13.4 7.3 %collective-permute-start.2 = (bf16[512,512]{1,0:T(8,128)(2,1)S(1)}, bf16[512,512]{1,0:T(8,128)(2,1)S(1)}, u32[]{:S(2)}, u32[]{:S(2)}) collective-permute-start(bf16[512,512]{1,0:T(8,128)(2,1)S(1)} %collective-permute-done.1.m2), channel_id=1, source_target_pairs={{0,32},{32,0},{64,96},{96,64},{128,160},{160,128},{192,224},{224,1... | collective-permute-start | bytes 1572872 | tf_op jit(solution)/shard_map/ppermute | solution.py:44
  20.7 1.9 %shard_map.50 = (s32[1,16]{1,0:T(1,128)S(4)}, bf16[512,512]{1,0:T(8,128)(2,1)S(1)}, bf16[4,4,64,128]{3,2,1,0:T(8,128)(2,1)}, bf16[4,4,64,128]{3,2,1,0:T(8,128)(2,1)S(1)}) custom-call(s32[1,16]{1,0:T(1,128)} %edge_in.1, bf16[512,512]{1,0:T(8,128)(2,1)} %bitcast.9, f32[512,256]{1,0:T(8,128)} %bitcast.6), custom_call_target="tpu_custom_call" | custom-call | tf_op jit(solution)/shard_map/pallas_call | solution.py:99
  22.6 0.0 copy-start.2
  22.6 0.7 copy-done.2
  23.3 3.4 %all-to-all-start = ((bf16[4,4,64,128]{3,2,1,0:T(8,128)(2,1)}), bf16[4,4,64,128]{3,2,1,0:T(8,128)(2,1)S(1)}, u32[]{:S(2)}, u32[]{:S(2)}) async-start(bf16[4,4,64,128]{3,2,1,0:T(8,128)(2,1)} %get-tuple-element.20), calls=%async_computation | async-start | bytes 524288 | tf_op jit(solution)/shard_map/all_to_all | solution.py:73
  26.7 0.0 collective-permute-done.m1
  26.7 0.7 shard_map.51
  27.5 0.0 copy-start
  27.5 1.0 %copy-done = bf16[2,4,128,512]{3,2,1,0:T(8,128)(2,1)} copy-done((bf16[2,4,128,512]{3,2,1,0:T(8,128)(2,1)}, bf16[2,4,128,512]{3,2,1,0:T(8,128)(2,1)S(1)}, u32[]{:S(2)}) %copy-start) | copy-done | bytes 1048600
  28.4 3.3 %all-to-all-done.given = bf16[4,4,64,128]{3,2,1,0:T(8,128)(2,1)S(1)} async-done(((bf16[4,4,64,128]{3,2,1,0:T(8,128)(2,1)}), bf16[4,4,64,128]{3,2,1,0:T(8,128)(2,1)S(1)}, u32[]{:S(2)}, u32[]{:S(2)}) %all-to-all-start) | async-done | bytes 262176 | tf_op jit(solution)/shard_map/all_to_all | solution.py:73
  31.7 0.0 collective-permute-done.2.m3
  31.7 3.5 %shard_map.54 = (bf16[4,2,64,128]{3,2,1,0:T(8,128)(2,1)S(1)}, bf16[4,2,64,128]{3,2,1,0:T(8,128)(2,1)S(1)}, bf16[2,512,512]{2,1,0:T(8,128)(2,1)S(1)}) custom-call(s32[1,16]{1,0:T(1,128)S(4)} %get-tuple-element.15.edge, bf16[2,512,512]{2,1,0:T(8,128)(2,1)S(1)} %get-tuple-element.19.here, bf16[512,512]{1,0:T(8,128)(2,1)S(1)} %collective-permute-done.1.m2, ...), custom_call_target="tpu_custom_call" | custom-call | tf_op jit(solution)/shard_map/pallas_call | solution.py:29
  35.2 0.0 copy-start.1
  35.3 3.2 %collective-permute-start.3 = (bf16[4,2,64,128]{3,2,1,0:T(8,128)(2,1)S(1)}, bf16[4,2,64,128]{3,2,1,0:T(8,128)(2,1)S(1)}, u32[]{:S(2)}, u32[]{:S(2)}) collective-permute-start(bf16[4,2,64,128]{3,2,1,0:T(8,128)(2,1)S(1)} %get-tuple-element.22), channel_id=1, source_target_pairs={{0,1},{1,0},{2,3},{3,2},{4,5},{5,4},{6,7},{7,6},{8,9},{9,8},{10,11... | collective-permute-start | bytes 393224 | tf_op jit(solution)/shard_map/ppermute | solution.py:57
  38.4 6.7 %collective-permute-start.4 = (bf16[4,2,64,128]{3,2,1,0:T(8,128)(2,1)S(1)}, bf16[4,2,64,128]{3,2,1,0:T(8,128)(2,1)S(1)}, u32[]{:S(2)}, u32[]{:S(2)}) collective-permute-start(bf16[4,2,64,128]{3,2,1,0:T(8,128)(2,1)S(1)} %get-tuple-element.23), channel_id=1, source_target_pairs={{1,2},{2,1},{3,4},{4,3},{5,6},{6,5},{7,8},{8,7},{9,10},{10,9},{11,... | collective-permute-start | bytes 393224 | tf_op jit(solution)/shard_map/ppermute | solution.py:57
  45.1 0.0 collective-permute-done.3.got_a
  45.1 2.3 %collective-permute-done.4.got_b = bf16[4,2,64,128]{3,2,1,0:T(8,128)(2,1)S(1)} collective-permute-done((bf16[4,2,64,128]{3,2,1,0:T(8,128)(2,1)S(1)}, bf16[4,2,64,128]{3,2,1,0:T(8,128)(2,1)S(1)}, u32[]{:S(2)}, u32[]{:S(2)}) %collective-permute-start.4) | collective-permute-done | bytes 131104 | tf_op jit(solution)/shard_map/ppermute | solution.py:57
  47.5 3.5 %shard_map.55 = (bf16[2,2,64,128]{3,2,1,0:T(8,128)(2,1)S(1)}, bf16[2,2,64,128]{3,2,1,0:T(8,128)(2,1)S(1)}, bf16[2,2,64,128]{3,2,1,0:T(8,128)(2,1)S(1)}, bf16[2,2,64,128]{3,2,1,0:T(8,128)(2,1)S(1)}) custom-call(s32[1,16]{1,0:T(1,128)S(4)} %get-tuple-element.15.edge, bf16[2,512,512]{2,1,0:T(8,128)(2,1)S(1)} %get-tuple-element.19.here, ...), custom_call_target="tpu_custom_call" | custom-call | tf_op jit(solution)/shard_map/pallas_call | solution.py:29
  51.0 1.9 %collective-permute-start.5 = (bf16[2,2,64,128]{3,2,1,0:T(8,128)(2,1)S(1)}, bf16[2,2,64,128]{3,2,1,0:T(8,128)(2,1)S(1)}, u32[]{:S(2)}, u32[]{:S(2)}) collective-permute-start(bf16[2,2,64,128]{3,2,1,0:T(8,128)(2,1)S(1)} %get-tuple-element.24), channel_id=1, source_target_pairs={{0,1},{1,0},{2,3},{3,2},{4,5},{5,4},{6,7},{7,6},{8,9},{9,8},{10,11... | collective-permute-start | bytes 196616 | tf_op jit(solution)/shard_map/ppermute | solution.py:57
  52.9 3.7 %collective-permute-start.6 = (bf16[2,2,64,128]{3,2,1,0:T(8,128)(2,1)S(1)}, bf16[2,2,64,128]{3,2,1,0:T(8,128)(2,1)S(1)}, u32[]{:S(2)}, u32[]{:S(2)}) collective-permute-start(bf16[2,2,64,128]{3,2,1,0:T(8,128)(2,1)S(1)} %get-tuple-element.25), channel_id=1, source_target_pairs={{0,65},{1,64},{2,67},{3,66},{4,69},{5,68},{6,71},{7,70},{8,73},{9,... | collective-permute-start | bytes 196616 | tf_op jit(solution)/shard_map/ppermute | solution.py:67
  56.7 6.6 %collective-permute-start.7 = (bf16[2,2,64,128]{3,2,1,0:T(8,128)(2,1)S(1)}, bf16[2,2,64,128]{3,2,1,0:T(8,128)(2,1)S(1)}, u32[]{:S(2)}, u32[]{:S(2)}) collective-permute-start(bf16[2,2,64,128]{3,2,1,0:T(8,128)(2,1)S(1)} %get-tuple-element.26), channel_id=1, source_target_pairs={{1,2},{2,1},{3,4},{4,3},{5,6},{6,5},{7,8},{8,7},{9,10},{10,9},{11,... | collective-permute-start | bytes 196616 | tf_op jit(solution)/shard_map/ppermute | solution.py:57
  63.3 2.5 %collective-permute-start.8 = (bf16[2,2,64,128]{3,2,1,0:T(8,128)(2,1)S(1)}, bf16[2,2,64,128]{3,2,1,0:T(8,128)(2,1)S(1)}, u32[]{:S(2)}, u32[]{:S(2)}) collective-permute-start(bf16[2,2,64,128]{3,2,1,0:T(8,128)(2,1)S(1)} %get-tuple-element.27), channel_id=1, source_target_pairs={{1,66},{2,65},{3,68},{4,67},{5,70},{6,69},{7,72},{8,71},{9,74},{10... | collective-permute-start | bytes 196616 | tf_op jit(solution)/shard_map/ppermute | solution.py:67
  65.8 0.0 collective-permute-done.5.n0
  65.8 0.0 collective-permute-done.6.n2
  65.8 0.0 collective-permute-done.7.f0
  65.8 6.7 %collective-permute-done.8.f2 = bf16[2,2,64,128]{3,2,1,0:T(8,128)(2,1)S(1)} collective-permute-done((bf16[2,2,64,128]{3,2,1,0:T(8,128)(2,1)S(1)}, bf16[2,2,64,128]{3,2,1,0:T(8,128)(2,1)S(1)}, u32[]{:S(2)}, u32[]{:S(2)}) %collective-permute-start.8) | collective-permute-done | bytes 65568 | tf_op jit(solution)/shard_map/ppermute | solution.py:67
  72.6 5.6 %collective-permute-start.9 = (bf16[2,4,64,128]{3,2,1,0:T(8,128)(2,1)S(1)}, bf16[2,4,64,128]{3,2,1,0:T(8,128)(2,1)S(1)}, u32[]{:S(2)}, u32[]{:S(2)}) collective-permute-start(bf16[2,4,64,128]{3,2,1,0:T(8,128)(2,1)S(1)} %shard_map.56), channel_id=1, source_target_pairs={{0,32},{32,0},{64,96},{96,64},{128,160},{160,128},{192,224},{224,1... | collective-permute-start | bytes 393224 | tf_op jit(solution)/shard_map/ppermute | solution.py:44
  78.2 0.0 copy-done.1
  78.2 2.1 %shard_map.52.source = bf16[16,128,512]{2,1,0:T(8,128)(2,1)S(1)} custom-call(s32[1,16]{1,0:T(1,128)S(4)} %get-tuple-element.15.edge, bf16[512,512]{1,0:T(8,128)(2,1)S(1)} %get-tuple-element.16.m0.own, bf16[512,512]{1,0:T(8,128)(2,1)S(1)} %collective-permute-done.m1, bf16[512,512]{1,0:T(8,128)(2,1)S(1)} %collective-permute-done.1.m2, ...), custom_call_target="tpu_custom_call" | custom-call | tf_op jit(solution)/shard_map/pallas_call | solution.py:29
  80.3 0.0 copy-start.3
  80.3 3.4 %shard_map.53 = bf16[16,128,512]{2,1,0:T(8,128)(2,1)} custom-call(s32[1,16]{1,0:T(1,128)S(4)} %get-tuple-element.15.edge, bf16[512,512]{1,0:T(8,128)(2,1)S(1)} %get-tuple-element.16.m0.own, bf16[512,512]{1,0:T(8,128)(2,1)S(1)} %collective-permute-done.m1, bf16[512,512]{1,0:T(8,128)(2,1)S(1)} %collective-permute-done.1.m2, ...), custom_call_target="tpu_custom_call" | custom-call | tf_op jit(solution)/shard_map/pallas_call | solution.py:314
  83.7 0.0 collective-permute-done.9.others
  83.7 0.0 copy-done.3
  83.7 1.2 %shard_map.57 = f32[512,256]{1,0:T(8,128)} custom-call(bf16[512,512]{1,0:T(8,128)(2,1)S(1)} %get-tuple-element.16.m0.own, bf16[4,4,64,128]{3,2,1,0:T(8,128)(2,1)S(1)} %copy-done.3, bf16[2,2,64,128]{3,2,1,0:T(8,128)(2,1)S(1)} %collective-permute-done.5.n0, bf16[2,2,64,128]{3,2,1,0:T(8,128)(2,1)S(1)} %collective-permute-done.6.n2, ...), custom_call_target="tpu_custom_call" | custom-call | tf_op jit(solution)/shard_map/pallas_call | solution.py:29
  (1 shorter events, 0.0 us)
Async XLA Ops:
  0.6 12.7 %collective-permute-start.1 = (bf16[512,512]{1,0:T(8,128)(2,1)}, bf16[512,512]{1,0:T(8,128)(2,1)S(1)}, u32[]{:S(2)}, u32[]{:S(2)}) collective-permute-start(bf16[512,512]{1,0:T(8,128)(2,1)} %bitcast.7), channel_id=1, source_target_pairs={{0,64},{32,96},{64,0},{96,32},{128,192},{160,224},{192,128},{224,1... | collective-permute-start | bytes 1572872 | tf_op jit(solution)/shard_map/ppermute | solution.py:44
  5.5 21.2 %collective-permute-start = (bf16[512,512]{1,0:T(8,128)(2,1)}, bf16[512,512]{1,0:T(8,128)(2,1)S(1)}, u32[]{:S(2)}, u32[]{:S(2)}) collective-permute-start(bf16[512,512]{1,0:T(8,128)(2,1)} %bitcast.8), channel_id=1, source_target_pairs={{0,32},{32,0},{64,96},{96,64},{128,160},{160,128},{192,224},{224,1... | collective-permute-start | bytes 1572872 | tf_op jit(solution)/shard_map/ppermute | solution.py:44
  13.4 18.3 %collective-permute-start.2 = (bf16[512,512]{1,0:T(8,128)(2,1)S(1)}, bf16[512,512]{1,0:T(8,128)(2,1)S(1)}, u32[]{:S(2)}, u32[]{:S(2)}) collective-permute-start(bf16[512,512]{1,0:T(8,128)(2,1)S(1)} %collective-permute-done.1.m2), channel_id=1, source_target_pairs={{0,32},{32,0},{64,96},{96,64},{128,160},{160,128},{192,224},{224,1... | collective-permute-start | bytes 1572872 | tf_op jit(solution)/shard_map/ppermute | solution.py:44
  22.6 0.7 copy-start.2
  23.3 8.4 %all-to-all-start = ((bf16[4,4,64,128]{3,2,1,0:T(8,128)(2,1)}), bf16[4,4,64,128]{3,2,1,0:T(8,128)(2,1)S(1)}, u32[]{:S(2)}, u32[]{:S(2)}) async-start(bf16[4,4,64,128]{3,2,1,0:T(8,128)(2,1)} %get-tuple-element.20), calls=%async_computation | async-start | bytes 524288 | tf_op jit(solution)/shard_map/all_to_all | solution.py:73
  27.5 1.0 %copy-start = (bf16[2,4,128,512]{3,2,1,0:T(8,128)(2,1)}, bf16[2,4,128,512]{3,2,1,0:T(8,128)(2,1)S(1)}, u32[]{:S(2)}) copy-start(bf16[2,4,128,512]{3,2,1,0:T(8,128)(2,1)S(1)} %get-tuple-element.17.begun) | copy-start | bytes 3145732
  35.2 42.9 %copy-start.1 = (bf16[2,4,128,512]{3,2,1,0:T(8,128)(2,1)S(1)}, bf16[2,4,128,512]{3,2,1,0:T(8,128)(2,1)}, u32[]{:S(2)}) copy-start(bf16[2,4,128,512]{3,2,1,0:T(8,128)(2,1)} %copy-done) | copy-start | bytes 3145732
  35.3 9.9 %collective-permute-start.3 = (bf16[4,2,64,128]{3,2,1,0:T(8,128)(2,1)S(1)}, bf16[4,2,64,128]{3,2,1,0:T(8,128)(2,1)S(1)}, u32[]{:S(2)}, u32[]{:S(2)}) collective-permute-start(bf16[4,2,64,128]{3,2,1,0:T(8,128)(2,1)S(1)} %get-tuple-element.22), channel_id=1, source_target_pairs={{0,1},{1,0},{2,3},{3,2},{4,5},{5,4},{6,7},{7,6},{8,9},{9,8},{10,11... | collective-permute-start | bytes 393224 | tf_op jit(solution)/shard_map/ppermute | solution.py:57
  38.4 9.0 %collective-permute-start.4 = (bf16[4,2,64,128]{3,2,1,0:T(8,128)(2,1)S(1)}, bf16[4,2,64,128]{3,2,1,0:T(8,128)(2,1)S(1)}, u32[]{:S(2)}, u32[]{:S(2)}) collective-permute-start(bf16[4,2,64,128]{3,2,1,0:T(8,128)(2,1)S(1)} %get-tuple-element.23), channel_id=1, source_target_pairs={{1,2},{2,1},{3,4},{4,3},{5,6},{6,5},{7,8},{8,7},{9,10},{10,9},{11,... | collective-permute-start | bytes 393224 | tf_op jit(solution)/shard_map/ppermute | solution.py:57
  51.0 14.8 %collective-permute-start.5 = (bf16[2,2,64,128]{3,2,1,0:T(8,128)(2,1)S(1)}, bf16[2,2,64,128]{3,2,1,0:T(8,128)(2,1)S(1)}, u32[]{:S(2)}, u32[]{:S(2)}) collective-permute-start(bf16[2,2,64,128]{3,2,1,0:T(8,128)(2,1)S(1)} %get-tuple-element.24), channel_id=1, source_target_pairs={{0,1},{1,0},{2,3},{3,2},{4,5},{5,4},{6,7},{7,6},{8,9},{9,8},{10,11... | collective-permute-start | bytes 196616 | tf_op jit(solution)/shard_map/ppermute | solution.py:57
  52.9 12.9 %collective-permute-start.6 = (bf16[2,2,64,128]{3,2,1,0:T(8,128)(2,1)S(1)}, bf16[2,2,64,128]{3,2,1,0:T(8,128)(2,1)S(1)}, u32[]{:S(2)}, u32[]{:S(2)}) collective-permute-start(bf16[2,2,64,128]{3,2,1,0:T(8,128)(2,1)S(1)} %get-tuple-element.25), channel_id=1, source_target_pairs={{0,65},{1,64},{2,67},{3,66},{4,69},{5,68},{6,71},{7,70},{8,73},{9,... | collective-permute-start | bytes 196616 | tf_op jit(solution)/shard_map/ppermute | solution.py:67
  56.7 9.2 %collective-permute-start.7 = (bf16[2,2,64,128]{3,2,1,0:T(8,128)(2,1)S(1)}, bf16[2,2,64,128]{3,2,1,0:T(8,128)(2,1)S(1)}, u32[]{:S(2)}, u32[]{:S(2)}) collective-permute-start(bf16[2,2,64,128]{3,2,1,0:T(8,128)(2,1)S(1)} %get-tuple-element.26), channel_id=1, source_target_pairs={{1,2},{2,1},{3,4},{4,3},{5,6},{6,5},{7,8},{8,7},{9,10},{10,9},{11,... | collective-permute-start | bytes 196616 | tf_op jit(solution)/shard_map/ppermute | solution.py:57
  63.3 9.2 %collective-permute-start.8 = (bf16[2,2,64,128]{3,2,1,0:T(8,128)(2,1)S(1)}, bf16[2,2,64,128]{3,2,1,0:T(8,128)(2,1)S(1)}, u32[]{:S(2)}, u32[]{:S(2)}) collective-permute-start(bf16[2,2,64,128]{3,2,1,0:T(8,128)(2,1)S(1)} %get-tuple-element.27), channel_id=1, source_target_pairs={{1,66},{2,65},{3,68},{4,67},{5,70},{6,69},{7,72},{8,71},{9,74},{10... | collective-permute-start | bytes 196616 | tf_op jit(solution)/shard_map/ppermute | solution.py:67
  72.6 11.2 %collective-permute-start.9 = (bf16[2,4,64,128]{3,2,1,0:T(8,128)(2,1)S(1)}, bf16[2,4,64,128]{3,2,1,0:T(8,128)(2,1)S(1)}, u32[]{:S(2)}, u32[]{:S(2)}) collective-permute-start(bf16[2,4,64,128]{3,2,1,0:T(8,128)(2,1)S(1)} %shard_map.56), channel_id=1, source_target_pairs={{0,32},{32,0},{64,96},{96,64},{128,160},{160,128},{192,224},{224,1... | collective-permute-start | bytes 393224 | tf_op jit(solution)/shard_map/ppermute | solution.py:44
  80.3 3.4 %copy-start.3 = (bf16[4,4,64,128]{3,2,1,0:T(8,128)(2,1)S(1)}, bf16[4,4,64,128]{3,2,1,0:T(8,128)(2,1)}, u32[]{:S(2)}) copy-start(bf16[4,4,64,128]{3,2,1,0:T(8,128)(2,1)} %copy-done.2) | copy-start | bytes 786436

commit v3 on v1

--- a/solution.py
+++ b/solution.py
@@ -107,12 +107,14 @@
     return block
 
 
-def chain(edge_ref, turned, base_block, store, z_ref):
+def chain(edge_ref, turned, base_block, store, z_ref, known=()):
     position = lax.axis_index("sub") % 4
     for step in range(KTERMS + 1):
         slot, before = step % 2, (step + 1) % 2
         for r in range(4):
             leaf = position ^ r
+            if step == 0 and r in known:
+                continue
             parts = []
             for i in range(4):
                 part = base_block(r, i)
@@ -120,7 +122,7 @@
                     part = part + z_ref[before, edge_ref[0, leaf * 4 + i]]
                 parts.append(part.astype(BF16))
             operand = jnp.concatenate(parts, 1)
-            out = jnp.dot(operand, turned[r], preferred_element_type=F32)
+            out = jnp.dot(operand, turned[r][...], preferred_element_type=F32)
             for i in range(4):
                 value = out[:, i * EDGE : (i + 1) * EDGE]
                 if step == KTERMS:
@@ -145,116 +147,183 @@
     return store
 
 
-def first_sweep_kernel(edge, m0, m1, m2, m3, given, to_a, to_b, turned, z):
+def products_kernel(here, m2, given, t2, begun):
+    position = lax.axis_index("sub") % 4
+    t2[...] = m2[...].T
+    for r, turned in enumerate((here.at[0], here.at[1], t2)):
+        v = jnp.concatenate([given[position ^ r, i] for i in range(4)], 1)
+        out = jnp.dot(v, turned[...], preferred_element_type=F32)
+        for i in range(4):
+            begun[r, i] = out[:, i * EDGE : (i + 1) * EDGE]
+
+
+def products(here, m2, given):
+    t2 = pltpu.VMEM(m2.shape, BF16)
+    begun = pltpu.VMEM((3,) + given.shape[1:], F32)
+    return call(products_kernel, (t2, begun), (here, m2, given))
+
+
+def first_sweep_kernel(edge, here, t2, begun, m3, given, to_a, to_b, t3, z):
     position, parity = lax.axis_index("sub") % 4, lax.axis_index("dom") % 2
-    for r, m in enumerate((m0, m1, m2, m3)):
-        turned[r] = m[...].T
+    t3[...] = m3[...].T
+    for r in range(3):
+        for i in range(4):
+            z[0, (position ^ r) * 4 + i] = begun[r, i]
     base = lambda r, i: given[position ^ r, i].astype(F32)
-    chain(edge, turned, base, send_store(to_a, to_b, parity), z)
-
-
-def next_sweep_kernel(edge, turned, given, got_a, got_b, to_a, to_b, v, z):
+    turned = (here.at[0], here.at[1], t2, t3)
+    chain(edge, turned, base, send_store(to_a, to_b, parity), z, (0, 1, 2))
+
+
+def next_sweep_kernel(edge, here, t2, t3, given, got_a, got_b, to_a, to_b, v, z):
     parity = lax.axis_index("dom") % 2
     block = swapped_in(given, got_a, got_b)
     for r in range(4):
         for i in range(4):
             v[r, i] = block(r, i).astype(BF16)
     base = lambda r, i: v[r, i].astype(F32)
+    turned = (here.at[0], here.at[1], t2, t3)
     chain(edge, turned, base, send_store(to_a, to_b, parity), z)
 
 
-def first_sweep(edge, maps, given):
+def first_sweep(edge, here, t2, begun, m3, given):
     _, blocks, width, _ = given.shape
     sent = pltpu.VMEM((4, blocks // 2, width, EDGE), BF16)
-    turned = pltpu.VMEM((4,) + maps[0].shape, BF16)
+    t3 = pltpu.VMEM(m3.shape, BF16)
     z = pltpu.VMEM((2, 4 * blocks, width, EDGE), F32)
-    return call(first_sweep_kernel, (sent, sent, turned), (*maps, given), (z,), edge)
-
-
-def next_sweep(edge, turned, given, got):
+    args = (here, t2, begun, m3, given)
+    return call(first_sweep_kernel, (sent, sent, t3), args, (z,), edge)
+
+
+def next_sweep(edge, here, t2, t3, given, got):
     _, blocks, width, _ = given.shape
     sent = pltpu.VMEM((4, blocks // 2, width, EDGE), BF16)
     v = pltpu.VMEM(given.shape, BF16)
     z = pltpu.VMEM((2, 4 * blocks, width, EDGE), F32)
-    return call(next_sweep_kernel, (sent, sent), (turned, given, *got), (v, z), edge)
-
-
-def join_kernel(given, got_a, got_b, out):
-    position = lax.axis_index("sub") % 4
+    return call(next_sweep_kernel, (sent, sent), (here, t2, t3, given, *got), (v, z), edge)
+
+
+def join_kernel(given, got_a, got_b, *out_refs):
     block = swapped_in(given, got_a, got_b)
     for r in range(4):
         for i in range(4):
-            out[position ^ r, i] = block(r, i).astype(BF16)
+            out_refs[r][i] = block(r, i).astype(BF16)
 
 
 def join(given, got):
-    return call(join_kernel, pltpu.VMEM(given.shape, BF16), (given, *got))
-
-
-def leaf_kernel(own, pieces, out, turned):
-    width = pieces.shape[2]
-    for k in range(4):
-        for i in range(4):
-            turned[k * width : (k + 1) * width, i * EDGE : (i + 1) * EDGE] = pieces[k, i]
+    return call(join_kernel, (pltpu.VMEM(given.shape[1:], BF16),) * 4, (given, *got))
+
+
+def leaf_kernel(own, u0, u1, u2, u3, out, turned):
+    position = lax.axis_index("sub") % 4
+    width = u0.shape[1]
+    for r, u in enumerate((u0, u1, u2, u3)):
+        rows = pl.ds(pl.multiple_of((position ^ r) * width, width), width)
+        for i in range(4):
+            turned[rows, i * EDGE : (i + 1) * EDGE] = u[i]
     out[...] = lax.dot_general(own[...], turned[...], NT, preferred_element_type=F32)
 
 
 def leaf_product(own, pieces):
-    _, blocks, width, _ = pieces.shape
+    blocks, width, _ = pieces[0].shape
     result = jax.ShapeDtypeStruct((own.shape[0], 4 * width), F32)
     turned = pltpu.VMEM((4 * width, blocks * EDGE), BF16)
-    return call(leaf_kernel, result, (own, pieces), (turned,))
-
-
-def apply_once(edge_ref, map_refs, source, target):
-    position = lax.axis_index("sub") % 4
+    return call(leaf_kernel, result, (own, *pieces), (turned,))
+
+
+def apply_leaf(edge_ref, map_refs, source, r):
+    leaf = (lax.axis_index("sub") % 4) ^ r
+    operand = jnp.concatenate([source[edge_ref[0, leaf * 4 + i]] for i in range(4)], 0)
+    out = jnp.dot(map_refs[r][...], operand, preferred_element_type=F32)
+    if r == 0:
+        out = out + map_refs[0][...].astype(F32)
+    return [out[i * EDGE : (i + 1) * EDGE].astype(BF16) for i in range(4)]
+
+
+def apply_once(edge_ref, map_refs, source, target, leaves=range(4)):
+    position = lax.axis_index("sub") % 4
+    for r in leaves:
+        for i, value in enumerate(apply_leaf(edge_ref, map_refs, source, r)):
+            target[(position ^ r) * 4 + i] = value
+
+
+def apply_some(edge_ref, map_refs, source, leaves, target):
+    for r in leaves:
+        for i, value in enumerate(apply_leaf(edge_ref, map_refs, source, r)):
+            target[r, i] = value
+
+
+def apply_first(edge_ref, m_ref, own_ref, r):
+    position = lax.axis_index("sub") % 4
+    parts = []
+    for i in range(4):
+        block = edge_ref[0, (position ^ r) * 4 + i]
+        rows = own_ref[pl.ds(pl.multiple_of(block % 4 * EDGE, EDGE), EDGE), :]
+        parts.append(jnp.where(block // 4 == position, rows, jnp.zeros_like(rows)))
+    out = jnp.dot(m_ref[...], jnp.concatenate(parts, 0), preferred_element_type=F32)
+    if r == 0:
+        out = out + own_ref[...].astype(F32)
+    return [out[i * EDGE : (i + 1) * EDGE].astype(BF16) for i in range(4)]
+
+
+def early_kernel(edge, m0, m1, here, begun):
+    for r, m in enumerate((m0, m1)):
+        here[r] = m[...].T
+        for i, value in enumerate(apply_first(edge, m, m0, r)):
+            begun[r, i] = value
+
+
+def early(edge, own, beside):
+    here = pltpu.VMEM((2,) + own.shape, BF16)
+    begun = pltpu.VMEM((2, 4, EDGE, own.shape[1]), BF16)
+    return call(early_kernel, (here, begun), (own, beside), (), edge)
+
+
+def merge_first_kernel(edge, m0, m1, m2, m3, begun, out, half, work):
+    maps = (m0, m1, m2, m3)
+    position = lax.axis_index("sub") % 4
+    for r in range(2):
+        for i in range(4):
+            work[(position ^ r) * 4 + i] = begun[r, i]
+    for r, m in ((2, m2), (3, m3)):
+        for i, value in enumerate(apply_first(edge, m, m0, r)):
+            work[(position ^ r) * 4 + i] = value
+    apply_once(edge, maps, work, out)
+    apply_some(edge, maps, out, (0, 1), half)
+
+
+def merge_last_kernel(edge, m0, m1, m2, m3, source, half, out, work, last, sems):
+    maps = (m0, m1, m2, m3)
+    position = lax.axis_index("sub") % 4
+    for r in range(2):
+        for i in range(4):
+            work[(position ^ r) * 4 + i] = half[r, i]
+    apply_once(edge, maps, source, work, (2, 3))
+    copies = []
     for r in range(4):
-        leaf = position ^ r
-        operand = jnp.concatenate([source[edge_ref[0, leaf * 4 + i]] for i in range(4)], 0)
-        out = jnp.dot(map_refs[r][...], operand, preferred_element_type=F32)
-        if r == 0:
-            out = out + map_refs[0][...].astype(F32)
-        for i in range(4):
-            target[leaf * 4 + i] = out[i * EDGE : (i + 1) * EDGE].astype(BF16)
-
-
-def merge_first_kernel(edge, m0, m1, m2, m3, out, work):
-    position = lax.axis_index("sub") % 4
-    out[...] = jnp.zeros_like(out)
-    for i in range(4):
-        out[position * 4 + i] = m0[i * EDGE : (i + 1) * EDGE]
-    apply_once(edge, (m0, m1, m2, m3), out, work)
-    apply_once(edge, (m0, m1, m2, m3), work, out)
-
-
-def merge_next_kernel(edge, m0, m1, m2, m3, source, out, work):
-    apply_once(edge, (m0, m1, m2, m3), source, work)
-    apply_once(edge, (m0, m1, m2, m3), work, out)
-
-
-def merge(edge, maps, source):
+        apply_once(edge, maps, work, last, (r,))
+        blocks = pl.ds((position ^ r) * 4, 4)
+        copies.append(pltpu.make_async_copy(last.at[blocks], out.at[blocks], sems.at[r]))
+        copies[-1].start()
+    for copy in copies:
+        copy.wait()
+
+
+def merge_first(edge, maps, begun):
     width = maps[0].shape[0]
     work = pltpu.VMEM((4 * width // EDGE, EDGE, width), BF16)
-    if source is None:
-        return call(merge_first_kernel, work, maps, (work,), edge)
-    return call(merge_next_kernel, work, (*maps, source), (work,), edge)
-
-
-def store_kernel(value, out, sem):
-    copy = pltpu.make_async_copy(value, out, sem)
-    copy.start()
-    copy.wait()
-
-
-def store(value):
+    half = pltpu.VMEM(begun.shape, BF16)
+    return call(merge_first_kernel, (work, half), (*maps, begun), (work,), edge)
+
+
+def merge_last(edge, maps, source, half):
     return pl.pallas_call(
-        store_kernel,
-        out_shape=jax.ShapeDtypeStruct(value.shape, value.dtype),
-        in_specs=[VMEM],
+        merge_last_kernel,
+        out_shape=jax.ShapeDtypeStruct(source.shape, BF16),
+        in_specs=[SMEM] + [VMEM] * 6,
         out_specs=pl.BlockSpec(memory_space=pltpu.HBM),
-        scratch_shapes=[pltpu.SemaphoreType.DMA],
-        compiler_params=pltpu.CompilerParams(vmem_limit_bytes=1 << 20),
-    )(value)
+        scratch_shapes=[pltpu.VMEM(source.shape, BF16)] * 2 + [pltpu.SemaphoreType.DMA((4,))],
+        compiler_params=pltpu.CompilerParams(vmem_limit_bytes=16 << 20),
+    )(edge, *maps, source, half)
 
 
 def per_device(leaf_maps, edge, incoming):
@@ -266,23 +335,26 @@
     across = sub_partner(own, 2)
     edge, own_near, mine = split_rhs(edge, own, incoming)
     beside = sub_partner(own, 1)
+    here, begun = early(edge, own_near, beside)
     given = group_exchange(mine)
     opposite = sub_partner(across, 1)
+    t2, first = products(here, across, given)
     maps = (own_near, beside, across, opposite)
 
     def swap(sent):
         far = dom_partner(sent[1], 1)
         return dom_partner(sent[0], 0), far
 
-    *sent, turned = first_sweep(edge, maps, given)
+    *sent, t3 = first_sweep(edge, here, t2, first, opposite, given)
     got = swap(sent)
-    merged = merge(edge, maps, None)
-    sent = next_sweep(edge, turned, given, got)
+    merged, half = merge_first(edge, maps, begun)
+    sent = next_sweep(edge, here, t2, t3, given, got)
     got = swap(sent)
-    merged = merge(edge, maps, merged)
+    merged = merge_last(edge, maps, merged, half)
     mine = join(given, got)
-    pieces = group_exchange(mine)
-    merged = store(merged)
+    pieces = [mine[0]]
+    for r in (1, 2, 3):
+        pieces.append(sub_partner(mine[r], r))
     leaf_out = leaf_product(own_near, pieces)
     return merged.reshape(1, 1, 4 * width, width), leaf_out[None, None]
 

time: 75.9 us -> 79.8 us (1.051)
  blocking collectives: 7.66 us -> 0 us
  starting transfers between devices: 43.3 us -> 50.6 us
  waiting for transfers between devices: 6.79 us -> 10.1 us
  local copies, waits for them, and re-layouts: 0 us -> 0.97 us
    ppermute x3 -> x6, starting transfers between devices: 17.9 us -> 28.8 us  [sub_partner(): lax.ppermute(value, 'sub', [(i, i ^ mask) for i in range(size)])]
    all_to_all x1 -> x0, blocking collectives: 7.66 us -> none  [group_exchange(): return near(lax.all_to_all(value, 'sub', 0, 0, axis_index_groups=groups))]
    all_to_all x1, starting transfers between devices: 6.99 us -> 3.41 us  [group_exchange(): return near(lax.all_to_all(value, 'sub', 0, 0, axis_index_groups=groups))]
    all_to_all x1, waiting for transfers between devices: 0.01 us -> 3.28 us  [group_exchange(): return near(lax.all_to_all(value, 'sub', 0, 0, axis_index_groups=groups))]
    pallas_call x6 -> x7, Pallas kernels: 14.4 us -> 12.1 us  [call(): pl.pallas_call(kernel, out_shape=results, in_specs=specs, out_specs=(VMEM...]
    pallas_call x1, Pallas kernels: 1.33 us -> 2.81 us  [merge_last(): pl.pallas_call(merge_last_kernel, out_shape=jax.ShapeDtypeStruct(source.s...]
    unnamed x0 -> x4, local copies, waits for them, and re-layouts: none -> 0.97 us
    ppermute x3 -> x6, waiting for transfers between devices: 2.06 us -> 2.07 us  [sub_partner(): lax.ppermute(value, 'sub', [(i, i ^ mask) for i in range(size)])]
  transfers between devices with their start and end apart: 8 -> 11, of which waited for: 3 -> 4; matrix products, arithmetic and copies ran while one was open for 0% -> 0% of each run, Pallas kernels for 10% -> 11%
where the time goes in v3:
time: 79.8 us; the launch traced here: 79.3 us
  starting transfers between devices  50.6 us (63%)
  Pallas kernels  16.8 us (21%)
  waiting for transfers between devices  10.1 us (13%)
  local copies, waits for them, and re-layouts  0.97 us (1%)
  between operations  0.85 us (1%)
    ppermute x6, starting transfers between devices, sub_partner(): lax.ppermute(value, 'sub', [(i, i ^ mask) for i in range(size)])  28.8 us
    ppermute x4, starting transfers between devices, dom_partner(): return near(lax.ppermute(value, 'dom', pairs))  18.4 us
    pallas_call x7, Pallas kernels, call(): pl.pallas_call(kernel, out_shape=results, in_specs=specs, out_specs=(VMEM...  12.1 us
    ppermute x4, waiting for transfers between devices, dom_partner(): return near(lax.ppermute(value, 'dom', pairs))  4.73 us
    all_to_all x1, starting transfers between devices, group_exchange(): return near(lax.all_to_all(value, 'sub', 0, 0, axis_index_groups=groups))  3.41 us
    all_to_all x1, waiting for transfers between devices, group_exchange(): return near(lax.all_to_all(value, 'sub', 0, 0, axis_index_groups=groups))  3.28 us
    pallas_call x1, Pallas kernels, merge_last(): pl.pallas_call(merge_last_kernel, out_shape=jax.ShapeDtypeStruct(source.s...  2.81 us
    ppermute x6, waiting for transfers between devices, sub_partner(): lax.ppermute(value, 'sub', [(i, i ^ mask) for i in range(size)])  2.07 us
  transfers between devices with their start and end apart: 11, of which 4 were waited for; matrix products, arithmetic and copies ran while one was open for 0% of the time, Pallas kernels for 11%

profile of v3, /device:TPU:1, one launch (start us, length us, event | category | flops | bytes accessed | tf_op | source)
XLA Modules:
  0.0 79.3 jit_solution(3355027368286062590)
XLA Ops:
  0.6 4.8 %collective-permute-start.1 = (bf16[512,512]{1,0:T(8,128)(2,1)}, bf16[512,512]{1,0:T(8,128)(2,1)S(1)}, u32[]{:S(2)}, u32[]{:S(2)}) collective-permute-start(bf16[512,512]{1,0:T(8,128)(2,1)} %bitcast.7), channel_id=1, source_target_pairs={{0,64},{32,96},{64,0},{96,32},{128,192},{160,224},{192,128},{224,1... | collective-permute-start | bytes 1572872 | tf_op jit(solution)/shard_map/ppermute | solution.py:44
  5.5 5.8 %collective-permute-start = (bf16[512,512]{1,0:T(8,128)(2,1)}, bf16[512,512]{1,0:T(8,128)(2,1)S(1)}, u32[]{:S(2)}, u32[]{:S(2)}) collective-permute-start(bf16[512,512]{1,0:T(8,128)(2,1)} %bitcast.8), channel_id=1, source_target_pairs={{0,32},{32,0},{64,96},{96,64},{128,160},{160,128},{192,224},{224,1... | collective-permute-start | bytes 1572872 | tf_op jit(solution)/shard_map/ppermute | solution.py:44
  11.3 2.1 %collective-permute-done.1.m2 = bf16[512,512]{1,0:T(8,128)(2,1)S(1)} collective-permute-done((bf16[512,512]{1,0:T(8,128)(2,1)}, bf16[512,512]{1,0:T(8,128)(2,1)S(1)}, u32[]{:S(2)}, u32[]{:S(2)}) %collective-permute-start.1) | collective-permute-done | bytes 524320 | tf_op jit(solution)/shard_map/ppermute | solution.py:44
  13.4 7.3 %collective-permute-start.2 = (bf16[512,512]{1,0:T(8,128)(2,1)S(1)}, bf16[512,512]{1,0:T(8,128)(2,1)S(1)}, u32[]{:S(2)}, u32[]{:S(2)}) collective-permute-start(bf16[512,512]{1,0:T(8,128)(2,1)S(1)} %collective-permute-done.1.m2), channel_id=1, source_target_pairs={{0,32},{32,0},{64,96},{96,64},{128,160},{160,128},{192,224},{224,1... | collective-permute-start | bytes 1572872 | tf_op jit(solution)/shard_map/ppermute | solution.py:44
  20.7 1.9 %shard_map.50 = (s32[1,16]{1,0:T(1,128)S(4)}, bf16[512,512]{1,0:T(8,128)(2,1)S(1)}, bf16[4,4,64,128]{3,2,1,0:T(8,128)(2,1)}) custom-call(s32[1,16]{1,0:T(1,128)} %edge_in.1, bf16[512,512]{1,0:T(8,128)(2,1)} %bitcast.9, f32[512,256]{1,0:T(8,128)} %bitcast.6), custom_call_target="tpu_custom_call" | custom-call | tf_op jit(solution)/shard_map/pallas_call | solution.py:82
  22.6 3.4 %all-to-all-start = ((bf16[4,4,64,128]{3,2,1,0:T(8,128)(2,1)}), bf16[4,4,64,128]{3,2,1,0:T(8,128)(2,1)S(1)}, u32[]{:S(2)}, u32[]{:S(2)}) async-start(bf16[4,4,64,128]{3,2,1,0:T(8,128)(2,1)} %get-tuple-element.25), calls=%async_computation | async-start | bytes 524288 | tf_op jit(solution)/shard_map/all_to_all | solution.py:59
  26.0 0.0 collective-permute-done.m1
  26.0 0.8 shard_map.51
  26.8 0.0 copy-start
  26.8 1.0 %copy-done = bf16[2,4,128,512]{3,2,1,0:T(8,128)(2,1)} copy-done((bf16[2,4,128,512]{3,2,1,0:T(8,128)(2,1)}, bf16[2,4,128,512]{3,2,1,0:T(8,128)(2,1)S(1)}, u32[]{:S(2)}) %copy-start) | copy-done | bytes 1048600
  27.8 3.3 %all-to-all-done.given = bf16[4,4,64,128]{3,2,1,0:T(8,128)(2,1)S(1)} async-done(((bf16[4,4,64,128]{3,2,1,0:T(8,128)(2,1)}), bf16[4,4,64,128]{3,2,1,0:T(8,128)(2,1)S(1)}, u32[]{:S(2)}, u32[]{:S(2)}) %all-to-all-start) | async-done | bytes 262176 | tf_op jit(solution)/shard_map/all_to_all | solution.py:59
  31.0 0.4 shard_map.54
  31.4 0.0 collective-permute-done.2.m3
  31.4 3.3 %shard_map.55 = (bf16[4,2,64,128]{3,2,1,0:T(8,128)(2,1)S(1)}, bf16[4,2,64,128]{3,2,1,0:T(8,128)(2,1)S(1)}, bf16[512,512]{1,0:T(8,128)(2,1)S(1)}) custom-call(s32[1,16]{1,0:T(1,128)S(4)} %get-tuple-element.20.edge, bf16[2,512,512]{2,1,0:T(8,128)(2,1)S(1)} %get-tuple-element.26.here, bf16[512,512]{1,0:T(8,128)(2,1)S(1)} %get-tuple-element.27.t2, ...), custom_call_target="tpu_custom_call" | custom-call | tf_op jit(solution)/shard_map/pallas_call | solution.py:29
  34.8 0.0 copy-start.1
  34.8 3.2 %collective-permute-start.3 = (bf16[4,2,64,128]{3,2,1,0:T(8,128)(2,1)S(1)}, bf16[4,2,64,128]{3,2,1,0:T(8,128)(2,1)S(1)}, u32[]{:S(2)}, u32[]{:S(2)}) collective-permute-start(bf16[4,2,64,128]{3,2,1,0:T(8,128)(2,1)S(1)} %get-tuple-element.30), channel_id=1, source_target_pairs={{0,1},{1,0},{2,3},{3,2},{4,5},{5,4},{6,7},{7,6},{8,9},{9,8},{10,11... | collective-permute-start | bytes 393224 | tf_op jit(solution)/shard_map/ppermute | solution.py:53
  38.0 6.7 %collective-permute-start.4 = (bf16[4,2,64,128]{3,2,1,0:T(8,128)(2,1)S(1)}, bf16[4,2,64,128]{3,2,1,0:T(8,128)(2,1)S(1)}, u32[]{:S(2)}, u32[]{:S(2)}) collective-permute-start(bf16[4,2,64,128]{3,2,1,0:T(8,128)(2,1)S(1)} %get-tuple-element.31), channel_id=1, source_target_pairs={{1,2},{2,1},{3,4},{4,3},{5,6},{6,5},{7,8},{8,7},{9,10},{10,9},{11,... | collective-permute-start | bytes 393224 | tf_op jit(solution)/shard_map/ppermute | solution.py:53
  44.6 0.0 collective-permute-done.3.got_a
  44.6 2.3 %collective-permute-done.4.got_b = bf16[4,2,64,128]{3,2,1,0:T(8,128)(2,1)S(1)} collective-permute-done((bf16[4,2,64,128]{3,2,1,0:T(8,128)(2,1)S(1)}, bf16[4,2,64,128]{3,2,1,0:T(8,128)(2,1)S(1)}, u32[]{:S(2)}, u32[]{:S(2)}) %collective-permute-start.4) | collective-permute-done | bytes 131104 | tf_op jit(solution)/shard_map/ppermute | solution.py:53
  47.0 3.5 %shard_map.56 = (bf16[4,2,64,128]{3,2,1,0:T(8,128)(2,1)S(1)}, bf16[4,2,64,128]{3,2,1,0:T(8,128)(2,1)S(1)}) custom-call(s32[1,16]{1,0:T(1,128)S(4)} %get-tuple-element.20.edge, bf16[2,512,512]{2,1,0:T(8,128)(2,1)S(1)} %get-tuple-element.26.here, bf16[512,512]{1,0:T(8,128)(2,1)S(1)} %get-tuple-element.27.t2, bf16[512,512]{1,0:T(8,128)(2,1)S(1)} %get-tuple-element.29.t3, ...), custom_call_target="tpu_custom_call" | custom-call | tf_op jit(solution)/shard_map/pallas_call | solution.py:29
  50.5 1.9 %collective-permute-start.5 = (bf16[4,2,64,128]{3,2,1,0:T(8,128)(2,1)S(1)}, bf16[4,2,64,128]{3,2,1,0:T(8,128)(2,1)S(1)}, u32[]{:S(2)}, u32[]{:S(2)}) collective-permute-start(bf16[4,2,64,128]{3,2,1,0:T(8,128)(2,1)S(1)} %get-tuple-element.32), channel_id=1, source_target_pairs={{0,1},{1,0},{2,3},{3,2},{4,5},{5,4},{6,7},{7,6},{8,9},{9,8},{10,11... | collective-permute-start | bytes 393224 | tf_op jit(solution)/shard_map/ppermute | solution.py:53
  52.4 6.6 %collective-permute-start.6 = (bf16[4,2,64,128]{3,2,1,0:T(8,128)(2,1)S(1)}, bf16[4,2,64,128]{3,2,1,0:T(8,128)(2,1)S(1)}, u32[]{:S(2)}, u32[]{:S(2)}) collective-permute-start(bf16[4,2,64,128]{3,2,1,0:T(8,128)(2,1)S(1)} %get-tuple-element.33), channel_id=1, source_target_pairs={{1,2},{2,1},{3,4},{4,3},{5,6},{6,5},{7,8},{8,7},{9,10},{10,9},{11,... | collective-permute-start | bytes 393224 | tf_op jit(solution)/shard_map/ppermute | solution.py:53
  59.1 0.0 collective-permute-done.5.got_a
  59.1 2.4 %collective-permute-done.6.got_b = bf16[4,2,64,128]{3,2,1,0:T(8,128)(2,1)S(1)} collective-permute-done((bf16[4,2,64,128]{3,2,1,0:T(8,128)(2,1)S(1)}, bf16[4,2,64,128]{3,2,1,0:T(8,128)(2,1)S(1)}, u32[]{:S(2)}, u32[]{:S(2)}) %collective-permute-start.6) | collective-permute-done | bytes 131104 | tf_op jit(solution)/shard_map/ppermute | solution.py:53
  61.5 0.1 shard_map.57
  61.6 5.4 %collective-permute-start.7 = (bf16[4,64,128]{2,1,0:T(8,128)(2,1)S(1)}, bf16[4,64,128]{2,1,0:T(8,128)(2,1)S(1)}, u32[]{:S(2)}, u32[]{:S(2)}) collective-permute-start(bf16[4,64,128]{2,1,0:T(8,128)(2,1)S(1)} %get-tuple-element.35), channel_id=1, source_target_pairs={{0,32},{32,0},{64,96},{96,64},{128,160},{160,128},{192,224},{224,1... | collective-permute-start | bytes 196616 | tf_op jit(solution)/shard_map/ppermute | solution.py:44
  66.9 2.0 %collective-permute-start.8 = (bf16[4,64,128]{2,1,0:T(8,128)(2,1)S(1)}, bf16[4,64,128]{2,1,0:T(8,128)(2,1)S(1)}, u32[]{:S(2)}, u32[]{:S(2)}) collective-permute-start(bf16[4,64,128]{2,1,0:T(8,128)(2,1)S(1)} %get-tuple-element.36), channel_id=1, source_target_pairs={{0,64},{32,96},{64,0},{96,32},{128,192},{160,224},{192,128},{224,1... | collective-permute-start | bytes 196616 | tf_op jit(solution)/shard_map/ppermute | solution.py:44
  68.9 3.5 %collective-permute-start.9 = (bf16[4,64,128]{2,1,0:T(8,128)(2,1)S(1)}, bf16[4,64,128]{2,1,0:T(8,128)(2,1)S(1)}, u32[]{:S(2)}, u32[]{:S(2)}) collective-permute-start(bf16[4,64,128]{2,1,0:T(8,128)(2,1)S(1)} %get-tuple-element.37), channel_id=1, source_target_pairs={{0,96},{32,64},{64,32},{96,0},{128,224},{160,192},{192,160},{224,1... | collective-permute-start | bytes 196616 | tf_op jit(solution)/shard_map/ppermute | solution.py:44
  72.4 0.0 copy-done.1
  72.4 2.8 %shard_map.52 = (bf16[16,128,512]{2,1,0:T(8,128)(2,1)S(1)}, bf16[2,4,128,512]{3,2,1,0:T(8,128)(2,1)S(1)}) custom-call(s32[1,16]{1,0:T(1,128)S(4)} %get-tuple-element.20.edge, bf16[512,512]{1,0:T(8,128)(2,1)S(1)} %get-tuple-element.21.m0.own, bf16[512,512]{1,0:T(8,128)(2,1)S(1)} %collective-permute-done.m1, bf16[512,512]{1,0:T(8,128)(2,1)S(1)} %collective-permute-done.1.m2, ...), custom_call_target="tpu_custom_call" | custom-call | tf_op jit(solution)/shard_map/pallas_call | solution.py:29
  75.3 2.8 %shard_map.53 = bf16[16,128,512]{2,1,0:T(8,128)(2,1)} custom-call(s32[1,16]{1,0:T(1,128)S(4)} %get-tuple-element.20.edge, bf16[512,512]{1,0:T(8,128)(2,1)S(1)} %get-tuple-element.21.m0.own, bf16[512,512]{1,0:T(8,128)(2,1)S(1)} %collective-permute-done.m1, bf16[512,512]{1,0:T(8,128)(2,1)S(1)} %collective-permute-done.1.m2, ...), custom_call_target="tpu_custom_call" | custom-call | tf_op jit(solution)/shard_map/pallas_call | solution.py:319
  78.1 0.0 collective-permute-done.7.u1
  78.1 0.0 collective-permute-done.8.u2
  78.1 0.0 collective-permute-done.9.u3
  78.1 1.2 %shard_map.58 = f32[512,256]{1,0:T(8,128)} custom-call(bf16[512,512]{1,0:T(8,128)(2,1)S(1)} %get-tuple-element.21.m0.own, bf16[4,64,128]{2,1,0:T(8,128)(2,1)S(1)} %get-tuple-element.34.u0, bf16[4,64,128]{2,1,0:T(8,128)(2,1)S(1)} %collective-permute-done.7.u1, bf16[4,64,128]{2,1,0:T(8,128)(2,1)S(1)} %collective-permute-done.8.u2, ...), custom_call_target="tpu_custom_call" | custom-call | tf_op jit(solution)/shard_map/pallas_call | solution.py:29
Async XLA Ops:
  0.6 12.7 %collective-permute-start.1 = (bf16[512,512]{1,0:T(8,128)(2,1)}, bf16[512,512]{1,0:T(8,128)(2,1)S(1)}, u32[]{:S(2)}, u32[]{:S(2)}) collective-permute-start(bf16[512,512]{1,0:T(8,128)(2,1)} %bitcast.7), channel_id=1, source_target_pairs={{0,64},{32,96},{64,0},{96,32},{128,192},{160,224},{192,128},{224,1... | collective-permute-start | bytes 1572872 | tf_op jit(solution)/shard_map/ppermute | solution.py:44
  5.5 20.6 %collective-permute-start = (bf16[512,512]{1,0:T(8,128)(2,1)}, bf16[512,512]{1,0:T(8,128)(2,1)S(1)}, u32[]{:S(2)}, u32[]{:S(2)}) collective-permute-start(bf16[512,512]{1,0:T(8,128)(2,1)} %bitcast.8), channel_id=1, source_target_pairs={{0,32},{32,0},{64,96},{96,64},{128,160},{160,128},{192,224},{224,1... | collective-permute-start | bytes 1572872 | tf_op jit(solution)/shard_map/ppermute | solution.py:44
  13.4 18.0 %collective-permute-start.2 = (bf16[512,512]{1,0:T(8,128)(2,1)S(1)}, bf16[512,512]{1,0:T(8,128)(2,1)S(1)}, u32[]{:S(2)}, u32[]{:S(2)}) collective-permute-start(bf16[512,512]{1,0:T(8,128)(2,1)S(1)} %collective-permute-done.1.m2), channel_id=1, source_target_pairs={{0,32},{32,0},{64,96},{96,64},{128,160},{160,128},{192,224},{224,1... | collective-permute-start | bytes 1572872 | tf_op jit(solution)/shard_map/ppermute | solution.py:44
  22.6 8.4 %all-to-all-start = ((bf16[4,4,64,128]{3,2,1,0:T(8,128)(2,1)}), bf16[4,4,64,128]{3,2,1,0:T(8,128)(2,1)S(1)}, u32[]{:S(2)}, u32[]{:S(2)}) async-start(bf16[4,4,64,128]{3,2,1,0:T(8,128)(2,1)} %get-tuple-element.25), calls=%async_computation | async-start | bytes 524288 | tf_op jit(solution)/shard_map/all_to_all | solution.py:59
  26.8 1.0 %copy-start = (bf16[2,4,128,512]{3,2,1,0:T(8,128)(2,1)}, bf16[2,4,128,512]{3,2,1,0:T(8,128)(2,1)S(1)}, u32[]{:S(2)}) copy-start(bf16[2,4,128,512]{3,2,1,0:T(8,128)(2,1)S(1)} %get-tuple-element.22.begun) | copy-start | bytes 3145732
  34.8 37.7 %copy-start.1 = (bf16[2,4,128,512]{3,2,1,0:T(8,128)(2,1)S(1)}, bf16[2,4,128,512]{3,2,1,0:T(8,128)(2,1)}, u32[]{:S(2)}) copy-start(bf16[2,4,128,512]{3,2,1,0:T(8,128)(2,1)} %copy-done) | copy-start | bytes 3145732
  34.8 9.9 %collective-permute-start.3 = (bf16[4,2,64,128]{3,2,1,0:T(8,128)(2,1)S(1)}, bf16[4,2,64,128]{3,2,1,0:T(8,128)(2,1)S(1)}, u32[]{:S(2)}, u32[]{:S(2)}) collective-permute-start(bf16[4,2,64,128]{3,2,1,0:T(8,128)(2,1)S(1)} %get-tuple-element.30), channel_id=1, source_target_pairs={{0,1},{1,0},{2,3},{3,2},{4,5},{5,4},{6,7},{7,6},{8,9},{9,8},{10,11... | collective-permute-start | bytes 393224 | tf_op jit(solution)/shard_map/ppermute | solution.py:53
  38.0 9.0 %collective-permute-start.4 = (bf16[4,2,64,128]{3,2,1,0:T(8,128)(2,1)S(1)}, bf16[4,2,64,128]{3,2,1,0:T(8,128)(2,1)S(1)}, u32[]{:S(2)}, u32[]{:S(2)}) collective-permute-start(bf16[4,2,64,128]{3,2,1,0:T(8,128)(2,1)S(1)} %get-tuple-element.31), channel_id=1, source_target_pairs={{1,2},{2,1},{3,4},{4,3},{5,6},{6,5},{7,8},{8,7},{9,10},{10,9},{11,... | collective-permute-start | bytes 393224 | tf_op jit(solution)/shard_map/ppermute | solution.py:53
  50.5 8.6 %collective-permute-start.5 = (bf16[4,2,64,128]{3,2,1,0:T(8,128)(2,1)S(1)}, bf16[4,2,64,128]{3,2,1,0:T(8,128)(2,1)S(1)}, u32[]{:S(2)}, u32[]{:S(2)}) collective-permute-start(bf16[4,2,64,128]{3,2,1,0:T(8,128)(2,1)S(1)} %get-tuple-element.32), channel_id=1, source_target_pairs={{0,1},{1,0},{2,3},{3,2},{4,5},{5,4},{6,7},{7,6},{8,9},{9,8},{10,11... | collective-permute-start | bytes 393224 | tf_op jit(solution)/shard_map/ppermute | solution.py:53
  52.4 9.0 %collective-permute-start.6 = (bf16[4,2,64,128]{3,2,1,0:T(8,128)(2,1)S(1)}, bf16[4,2,64,128]{3,2,1,0:T(8,128)(2,1)S(1)}, u32[]{:S(2)}, u32[]{:S(2)}) collective-permute-start(bf16[4,2,64,128]{3,2,1,0:T(8,128)(2,1)S(1)} %get-tuple-element.33), channel_id=1, source_target_pairs={{1,2},{2,1},{3,4},{4,3},{5,6},{6,5},{7,8},{8,7},{9,10},{10,9},{11,... | collective-permute-start | bytes 393224 | tf_op jit(solution)/shard_map/ppermute | solution.py:53
  61.6 16.5 %collective-permute-start.7 = (bf16[4,64,128]{2,1,0:T(8,128)(2,1)S(1)}, bf16[4,64,128]{2,1,0:T(8,128)(2,1)S(1)}, u32[]{:S(2)}, u32[]{:S(2)}) collective-permute-start(bf16[4,64,128]{2,1,0:T(8,128)(2,1)S(1)} %get-tuple-element.35), channel_id=1, source_target_pairs={{0,32},{32,0},{64,96},{96,64},{128,160},{160,128},{192,224},{224,1... | collective-permute-start | bytes 196616 | tf_op jit(solution)/shard_map/ppermute | solution.py:44
  66.9 11.2 %collective-permute-start.8 = (bf16[4,64,128]{2,1,0:T(8,128)(2,1)S(1)}, bf16[4,64,128]{2,1,0:T(8,128)(2,1)S(1)}, u32[]{:S(2)}, u32[]{:S(2)}) collective-permute-start(bf16[4,64,128]{2,1,0:T(8,128)(2,1)S(1)} %get-tuple-element.36), channel_id=1, source_target_pairs={{0,64},{32,96},{64,0},{96,32},{128,192},{160,224},{192,128},{224,1... | collective-permute-start | bytes 196616 | tf_op jit(solution)/shard_map/ppermute | solution.py:44
  68.9 9.2 %collective-permute-start.9 = (bf16[4,64,128]{2,1,0:T(8,128)(2,1)S(1)}, bf16[4,64,128]{2,1,0:T(8,128)(2,1)S(1)}, u32[]{:S(2)}, u32[]{:S(2)}) collective-permute-start(bf16[4,64,128]{2,1,0:T(8,128)(2,1)S(1)} %get-tuple-element.37), channel_id=1, source_target_pairs={{0,96},{32,64},{64,32},{96,0},{128,224},{160,192},{192,160},{224,1... | collective-permute-start | bytes 196616 | tf_op jit(solution)/shard_map/ppermute | solution.py:44

commit v4 on v3

--- a/solution.py
+++ b/solution.py
@@ -111,24 +111,26 @@
     position = lax.axis_index("sub") % 4
     for step in range(KTERMS + 1):
         slot, before = step % 2, (step + 1) % 2
-        for r in range(4):
-            leaf = position ^ r
-            if step == 0 and r in known:
-                continue
+        leaves = [r for r in range(4) if step > 0 or r not in known]
+        operands = {}
+        for r in leaves:
             parts = []
             for i in range(4):
                 part = base_block(r, i)
                 if step > 0:
-                    part = part + z_ref[before, edge_ref[0, leaf * 4 + i]]
+                    part = part + z_ref[before, edge_ref[0, (position ^ r) * 4 + i]]
                 parts.append(part.astype(BF16))
-            operand = jnp.concatenate(parts, 1)
-            out = jnp.dot(operand, turned[r][...], preferred_element_type=F32)
+            operands[r] = jnp.concatenate(parts, 1)
+        outs = {
+            r: jnp.dot(operands[r], turned[r][...], preferred_element_type=F32) for r in leaves
+        }
+        for r in leaves:
             for i in range(4):
-                value = out[:, i * EDGE : (i + 1) * EDGE]
+                value = outs[r][:, i * EDGE : (i + 1) * EDGE]
                 if step == KTERMS:
                     store(r, i, value)
                 else:
-                    z_ref[slot, leaf * 4 + i] = value
+                    z_ref[slot, (position ^ r) * 4 + i] = value
 
 
 def send_store(to_a, to_b, parity):

time: 79.8 us -> 77.7 us (0.974)
  Pallas kernels: 16.8 us -> 14.7 us
    pallas_call x7, Pallas kernels: 12.1 us -> 9.95 us  [call(): pl.pallas_call(kernel, out_shape=results, in_specs=specs, out_specs=(VMEM...]
where the time goes in v4:
time: 77.7 us; the launch traced here: 77.2 us
  starting transfers between devices  50.6 us (65%)
  Pallas kernels  14.7 us (19%)
  waiting for transfers between devices  10.1 us (13%)
  local copies, waits for them, and re-layouts  0.97 us (1%)
  between operations  0.85 us (1%)
    ppermute x6, starting transfers between devices, sub_partner(): lax.ppermute(value, 'sub', [(i, i ^ mask) for i in range(size)])  28.8 us
    ppermute x4, starting transfers between devices, dom_partner(): return near(lax.ppermute(value, 'dom', pairs))  18.4 us
    pallas_call x7, Pallas kernels, call(): pl.pallas_call(kernel, out_shape=results, in_specs=specs, out_specs=(VMEM...  9.95 us
    ppermute x4, waiting for transfers between devices, dom_partner(): return near(lax.ppermute(value, 'dom', pairs))  4.76 us
    all_to_all x1, starting transfers between devices, group_exchange(): return near(lax.all_to_all(value, 'sub', 0, 0, axis_index_groups=groups))  3.41 us
    all_to_all x1, waiting for transfers between devices, group_exchange(): return near(lax.all_to_all(value, 'sub', 0, 0, axis_index_groups=groups))  3.28 us
    pallas_call x1, Pallas kernels, merge_last(): pl.pallas_call(merge_last_kernel, out_shape=jax.ShapeDtypeStruct(source.s...  2.82 us
    ppermute x6, waiting for transfers between devices, sub_partner(): lax.ppermute(value, 'sub', [(i, i ^ mask) for i in range(size)])  2.07 us
  transfers between devices with their start and end apart: 11, of which 4 were waited for; matrix products, arithmetic and copies ran while one was open for 0% of the time, Pallas kernels for 11%

profile of v4, /device:TPU:1, one launch (start us, length us, event | category | flops | bytes accessed | tf_op | source)
XLA Modules:
  0.0 77.2 jit_solution(11471361181834759284)
XLA Ops:
  0.6 4.8 %collective-permute-start.1 = (bf16[512,512]{1,0:T(8,128)(2,1)}, bf16[512,512]{1,0:T(8,128)(2,1)S(1)}, u32[]{:S(2)}, u32[]{:S(2)}) collective-permute-start(bf16[512,512]{1,0:T(8,128)(2,1)} %bitcast.7), channel_id=1, source_target_pairs={{0,64},{32,96},{64,0},{96,32},{128,192},{160,224},{192,128},{224,1... | collective-permute-start | bytes 1572872 | tf_op jit(solution)/shard_map/ppermute | solution.py:44
  5.5 5.8 %collective-permute-start = (bf16[512,512]{1,0:T(8,128)(2,1)}, bf16[512,512]{1,0:T(8,128)(2,1)S(1)}, u32[]{:S(2)}, u32[]{:S(2)}) collective-permute-start(bf16[512,512]{1,0:T(8,128)(2,1)} %bitcast.8), channel_id=1, source_target_pairs={{0,32},{32,0},{64,96},{96,64},{128,160},{160,128},{192,224},{224,1... | collective-permute-start | bytes 1572872 | tf_op jit(solution)/shard_map/ppermute | solution.py:44
  11.3 2.1 %collective-permute-done.1.m2 = bf16[512,512]{1,0:T(8,128)(2,1)S(1)} collective-permute-done((bf16[512,512]{1,0:T(8,128)(2,1)}, bf16[512,512]{1,0:T(8,128)(2,1)S(1)}, u32[]{:S(2)}, u32[]{:S(2)}) %collective-permute-start.1) | collective-permute-done | bytes 524320 | tf_op jit(solution)/shard_map/ppermute | solution.py:44
  13.4 7.3 %collective-permute-start.2 = (bf16[512,512]{1,0:T(8,128)(2,1)S(1)}, bf16[512,512]{1,0:T(8,128)(2,1)S(1)}, u32[]{:S(2)}, u32[]{:S(2)}) collective-permute-start(bf16[512,512]{1,0:T(8,128)(2,1)S(1)} %collective-permute-done.1.m2), channel_id=1, source_target_pairs={{0,32},{32,0},{64,96},{96,64},{128,160},{160,128},{192,224},{224,1... | collective-permute-start | bytes 1572872 | tf_op jit(solution)/shard_map/ppermute | solution.py:44
  20.7 1.9 %shard_map.50 = (s32[1,16]{1,0:T(1,128)S(4)}, bf16[512,512]{1,0:T(8,128)(2,1)S(1)}, bf16[4,4,64,128]{3,2,1,0:T(8,128)(2,1)}) custom-call(s32[1,16]{1,0:T(1,128)} %edge_in.1, bf16[512,512]{1,0:T(8,128)(2,1)} %bitcast.9, f32[512,256]{1,0:T(8,128)} %bitcast.6), custom_call_target="tpu_custom_call" | custom-call | tf_op jit(solution)/shard_map/pallas_call | solution.py:82
  22.6 3.4 %all-to-all-start = ((bf16[4,4,64,128]{3,2,1,0:T(8,128)(2,1)}), bf16[4,4,64,128]{3,2,1,0:T(8,128)(2,1)S(1)}, u32[]{:S(2)}, u32[]{:S(2)}) async-start(bf16[4,4,64,128]{3,2,1,0:T(8,128)(2,1)} %get-tuple-element.25), calls=%async_computation | async-start | bytes 524288 | tf_op jit(solution)/shard_map/all_to_all | solution.py:59
  26.0 0.0 collective-permute-done.m1
  26.0 0.8 shard_map.51
  26.8 0.0 copy-start
  26.8 1.0 %copy-done = bf16[2,4,128,512]{3,2,1,0:T(8,128)(2,1)} copy-done((bf16[2,4,128,512]{3,2,1,0:T(8,128)(2,1)}, bf16[2,4,128,512]{3,2,1,0:T(8,128)(2,1)S(1)}, u32[]{:S(2)}) %copy-start) | copy-done | bytes 1048600
  27.8 3.3 %all-to-all-done.given = bf16[4,4,64,128]{3,2,1,0:T(8,128)(2,1)S(1)} async-done(((bf16[4,4,64,128]{3,2,1,0:T(8,128)(2,1)}), bf16[4,4,64,128]{3,2,1,0:T(8,128)(2,1)S(1)}, u32[]{:S(2)}, u32[]{:S(2)}) %all-to-all-start) | async-done | bytes 262176 | tf_op jit(solution)/shard_map/all_to_all | solution.py:59
  31.0 0.4 shard_map.54
  31.4 0.0 collective-permute-done.2.m3
  31.4 2.3 %shard_map.55 = (bf16[4,2,64,128]{3,2,1,0:T(8,128)(2,1)S(1)}, bf16[4,2,64,128]{3,2,1,0:T(8,128)(2,1)S(1)}, bf16[512,512]{1,0:T(8,128)(2,1)S(1)}) custom-call(s32[1,16]{1,0:T(1,128)S(4)} %get-tuple-element.20.edge, bf16[2,512,512]{2,1,0:T(8,128)(2,1)S(1)} %get-tuple-element.26.here, bf16[512,512]{1,0:T(8,128)(2,1)S(1)} %get-tuple-element.27.t2, ...), custom_call_target="tpu_custom_call" | custom-call | tf_op jit(solution)/shard_map/pallas_call | solution.py:29
  33.7 0.0 copy-start.1
  33.7 3.2 %collective-permute-start.3 = (bf16[4,2,64,128]{3,2,1,0:T(8,128)(2,1)S(1)}, bf16[4,2,64,128]{3,2,1,0:T(8,128)(2,1)S(1)}, u32[]{:S(2)}, u32[]{:S(2)}) collective-permute-start(bf16[4,2,64,128]{3,2,1,0:T(8,128)(2,1)S(1)} %get-tuple-element.30), channel_id=1, source_target_pairs={{0,1},{1,0},{2,3},{3,2},{4,5},{5,4},{6,7},{7,6},{8,9},{9,8},{10,11... | collective-permute-start | bytes 393224 | tf_op jit(solution)/shard_map/ppermute | solution.py:53
  36.9 6.6 %collective-permute-start.4 = (bf16[4,2,64,128]{3,2,1,0:T(8,128)(2,1)S(1)}, bf16[4,2,64,128]{3,2,1,0:T(8,128)(2,1)S(1)}, u32[]{:S(2)}, u32[]{:S(2)}) collective-permute-start(bf16[4,2,64,128]{3,2,1,0:T(8,128)(2,1)S(1)} %get-tuple-element.31), channel_id=1, source_target_pairs={{1,2},{2,1},{3,4},{4,3},{5,6},{6,5},{7,8},{8,7},{9,10},{10,9},{11,... | collective-permute-start | bytes 393224 | tf_op jit(solution)/shard_map/ppermute | solution.py:53
  43.6 0.0 collective-permute-done.3.got_a
  43.6 2.4 %collective-permute-done.4.got_b = bf16[4,2,64,128]{3,2,1,0:T(8,128)(2,1)S(1)} collective-permute-done((bf16[4,2,64,128]{3,2,1,0:T(8,128)(2,1)S(1)}, bf16[4,2,64,128]{3,2,1,0:T(8,128)(2,1)S(1)}, u32[]{:S(2)}, u32[]{:S(2)}) %collective-permute-start.4) | collective-permute-done | bytes 131104 | tf_op jit(solution)/shard_map/ppermute | solution.py:53
  46.0 2.4 %shard_map.56 = (bf16[4,2,64,128]{3,2,1,0:T(8,128)(2,1)S(1)}, bf16[4,2,64,128]{3,2,1,0:T(8,128)(2,1)S(1)}) custom-call(s32[1,16]{1,0:T(1,128)S(4)} %get-tuple-element.20.edge, bf16[2,512,512]{2,1,0:T(8,128)(2,1)S(1)} %get-tuple-element.26.here, bf16[512,512]{1,0:T(8,128)(2,1)S(1)} %get-tuple-element.27.t2, bf16[512,512]{1,0:T(8,128)(2,1)S(1)} %get-tuple-element.29.t3, ...), custom_call_target="tpu_custom_call" | custom-call | tf_op jit(solution)/shard_map/pallas_call | solution.py:29
  48.4 1.9 %collective-permute-start.5 = (bf16[4,2,64,128]{3,2,1,0:T(8,128)(2,1)S(1)}, bf16[4,2,64,128]{3,2,1,0:T(8,128)(2,1)S(1)}, u32[]{:S(2)}, u32[]{:S(2)}) collective-permute-start(bf16[4,2,64,128]{3,2,1,0:T(8,128)(2,1)S(1)} %get-tuple-element.32), channel_id=1, source_target_pairs={{0,1},{1,0},{2,3},{3,2},{4,5},{5,4},{6,7},{7,6},{8,9},{9,8},{10,11... | collective-permute-start | bytes 393224 | tf_op jit(solution)/shard_map/ppermute | solution.py:53
  50.3 6.6 %collective-permute-start.6 = (bf16[4,2,64,128]{3,2,1,0:T(8,128)(2,1)S(1)}, bf16[4,2,64,128]{3,2,1,0:T(8,128)(2,1)S(1)}, u32[]{:S(2)}, u32[]{:S(2)}) collective-permute-start(bf16[4,2,64,128]{3,2,1,0:T(8,128)(2,1)S(1)} %get-tuple-element.33), channel_id=1, source_target_pairs={{1,2},{2,1},{3,4},{4,3},{5,6},{6,5},{7,8},{8,7},{9,10},{10,9},{11,... | collective-permute-start | bytes 393224 | tf_op jit(solution)/shard_map/ppermute | solution.py:53
  57.0 0.0 collective-permute-done.5.got_a
  57.0 2.4 %collective-permute-done.6.got_b = bf16[4,2,64,128]{3,2,1,0:T(8,128)(2,1)S(1)} collective-permute-done((bf16[4,2,64,128]{3,2,1,0:T(8,128)(2,1)S(1)}, bf16[4,2,64,128]{3,2,1,0:T(8,128)(2,1)S(1)}, u32[]{:S(2)}, u32[]{:S(2)}) %collective-permute-start.6) | collective-permute-done | bytes 131104 | tf_op jit(solution)/shard_map/ppermute | solution.py:53
  59.4 0.1 shard_map.57
  59.5 5.4 %collective-permute-start.7 = (bf16[4,64,128]{2,1,0:T(8,128)(2,1)S(1)}, bf16[4,64,128]{2,1,0:T(8,128)(2,1)S(1)}, u32[]{:S(2)}, u32[]{:S(2)}) collective-permute-start(bf16[4,64,128]{2,1,0:T(8,128)(2,1)S(1)} %get-tuple-element.35), channel_id=1, source_target_pairs={{0,32},{32,0},{64,96},{96,64},{128,160},{160,128},{192,224},{224,1... | collective-permute-start | bytes 196616 | tf_op jit(solution)/shard_map/ppermute | solution.py:44
  64.8 2.0 %collective-permute-start.8 = (bf16[4,64,128]{2,1,0:T(8,128)(2,1)S(1)}, bf16[4,64,128]{2,1,0:T(8,128)(2,1)S(1)}, u32[]{:S(2)}, u32[]{:S(2)}) collective-permute-start(bf16[4,64,128]{2,1,0:T(8,128)(2,1)S(1)} %get-tuple-element.36), channel_id=1, source_target_pairs={{0,64},{32,96},{64,0},{96,32},{128,192},{160,224},{192,128},{224,1... | collective-permute-start | bytes 196616 | tf_op jit(solution)/shard_map/ppermute | solution.py:44
  66.8 3.5 %collective-permute-start.9 = (bf16[4,64,128]{2,1,0:T(8,128)(2,1)S(1)}, bf16[4,64,128]{2,1,0:T(8,128)(2,1)S(1)}, u32[]{:S(2)}, u32[]{:S(2)}) collective-permute-start(bf16[4,64,128]{2,1,0:T(8,128)(2,1)S(1)} %get-tuple-element.37), channel_id=1, source_target_pairs={{0,96},{32,64},{64,32},{96,0},{128,224},{160,192},{192,160},{224,1... | collective-permute-start | bytes 196616 | tf_op jit(solution)/shard_map/ppermute | solution.py:44
  70.3 0.0 copy-done.1
  70.3 2.8 %shard_map.52 = (bf16[16,128,512]{2,1,0:T(8,128)(2,1)S(1)}, bf16[2,4,128,512]{3,2,1,0:T(8,128)(2,1)S(1)}) custom-call(s32[1,16]{1,0:T(1,128)S(4)} %get-tuple-element.20.edge, bf16[512,512]{1,0:T(8,128)(2,1)S(1)} %get-tuple-element.21.m0.own, bf16[512,512]{1,0:T(8,128)(2,1)S(1)} %collective-permute-done.m1, bf16[512,512]{1,0:T(8,128)(2,1)S(1)} %collective-permute-done.1.m2, ...), custom_call_target="tpu_custom_call" | custom-call | tf_op jit(solution)/shard_map/pallas_call | solution.py:29
  73.2 2.8 %shard_map.53 = bf16[16,128,512]{2,1,0:T(8,128)(2,1)} custom-call(s32[1,16]{1,0:T(1,128)S(4)} %get-tuple-element.20.edge, bf16[512,512]{1,0:T(8,128)(2,1)S(1)} %get-tuple-element.21.m0.own, bf16[512,512]{1,0:T(8,128)(2,1)S(1)} %collective-permute-done.m1, bf16[512,512]{1,0:T(8,128)(2,1)S(1)} %collective-permute-done.1.m2, ...), custom_call_target="tpu_custom_call" | custom-call | tf_op jit(solution)/shard_map/pallas_call | solution.py:321
  76.0 0.0 collective-permute-done.7.u1
  76.0 0.0 collective-permute-done.8.u2
  76.0 0.0 collective-permute-done.9.u3
  76.0 1.2 %shard_map.58 = f32[512,256]{1,0:T(8,128)} custom-call(bf16[512,512]{1,0:T(8,128)(2,1)S(1)} %get-tuple-element.21.m0.own, bf16[4,64,128]{2,1,0:T(8,128)(2,1)S(1)} %get-tuple-element.34.u0, bf16[4,64,128]{2,1,0:T(8,128)(2,1)S(1)} %collective-permute-done.7.u1, bf16[4,64,128]{2,1,0:T(8,128)(2,1)S(1)} %collective-permute-done.8.u2, ...), custom_call_target="tpu_custom_call" | custom-call | tf_op jit(solution)/shard_map/pallas_call | solution.py:29
Async XLA Ops:
  0.6 12.7 %collective-permute-start.1 = (bf16[512,512]{1,0:T(8,128)(2,1)}, bf16[512,512]{1,0:T(8,128)(2,1)S(1)}, u32[]{:S(2)}, u32[]{:S(2)}) collective-permute-start(bf16[512,512]{1,0:T(8,128)(2,1)} %bitcast.7), channel_id=1, source_target_pairs={{0,64},{32,96},{64,0},{96,32},{128,192},{160,224},{192,128},{224,1... | collective-permute-start | bytes 1572872 | tf_op jit(solution)/shard_map/ppermute | solution.py:44
  5.5 20.6 %collective-permute-start = (bf16[512,512]{1,0:T(8,128)(2,1)}, bf16[512,512]{1,0:T(8,128)(2,1)S(1)}, u32[]{:S(2)}, u32[]{:S(2)}) collective-permute-start(bf16[512,512]{1,0:T(8,128)(2,1)} %bitcast.8), channel_id=1, source_target_pairs={{0,32},{32,0},{64,96},{96,64},{128,160},{160,128},{192,224},{224,1... | collective-permute-start | bytes 1572872 | tf_op jit(solution)/shard_map/ppermute | solution.py:44
  13.4 18.0 %collective-permute-start.2 = (bf16[512,512]{1,0:T(8,128)(2,1)S(1)}, bf16[512,512]{1,0:T(8,128)(2,1)S(1)}, u32[]{:S(2)}, u32[]{:S(2)}) collective-permute-start(bf16[512,512]{1,0:T(8,128)(2,1)S(1)} %collective-permute-done.1.m2), channel_id=1, source_target_pairs={{0,32},{32,0},{64,96},{96,64},{128,160},{160,128},{192,224},{224,1... | collective-permute-start | bytes 1572872 | tf_op jit(solution)/shard_map/ppermute | solution.py:44
  22.6 8.4 %all-to-all-start = ((bf16[4,4,64,128]{3,2,1,0:T(8,128)(2,1)}), bf16[4,4,64,128]{3,2,1,0:T(8,128)(2,1)S(1)}, u32[]{:S(2)}, u32[]{:S(2)}) async-start(bf16[4,4,64,128]{3,2,1,0:T(8,128)(2,1)} %get-tuple-element.25), calls=%async_computation | async-start | bytes 524288 | tf_op jit(solution)/shard_map/all_to_all | solution.py:59
  26.8 1.0 %copy-start = (bf16[2,4,128,512]{3,2,1,0:T(8,128)(2,1)}, bf16[2,4,128,512]{3,2,1,0:T(8,128)(2,1)S(1)}, u32[]{:S(2)}) copy-start(bf16[2,4,128,512]{3,2,1,0:T(8,128)(2,1)S(1)} %get-tuple-element.22.begun) | copy-start | bytes 3145732
  33.7 36.6 %copy-start.1 = (bf16[2,4,128,512]{3,2,1,0:T(8,128)(2,1)S(1)}, bf16[2,4,128,512]{3,2,1,0:T(8,128)(2,1)}, u32[]{:S(2)}) copy-start(bf16[2,4,128,512]{3,2,1,0:T(8,128)(2,1)} %copy-done) | copy-start | bytes 3145732
  33.7 9.9 %collective-permute-start.3 = (bf16[4,2,64,128]{3,2,1,0:T(8,128)(2,1)S(1)}, bf16[4,2,64,128]{3,2,1,0:T(8,128)(2,1)S(1)}, u32[]{:S(2)}, u32[]{:S(2)}) collective-permute-start(bf16[4,2,64,128]{3,2,1,0:T(8,128)(2,1)S(1)} %get-tuple-element.30), channel_id=1, source_target_pairs={{0,1},{1,0},{2,3},{3,2},{4,5},{5,4},{6,7},{7,6},{8,9},{9,8},{10,11... | collective-permute-start | bytes 393224 | tf_op jit(solution)/shard_map/ppermute | solution.py:53
  36.9 9.0 %collective-permute-start.4 = (bf16[4,2,64,128]{3,2,1,0:T(8,128)(2,1)S(1)}, bf16[4,2,64,128]{3,2,1,0:T(8,128)(2,1)S(1)}, u32[]{:S(2)}, u32[]{:S(2)}) collective-permute-start(bf16[4,2,64,128]{3,2,1,0:T(8,128)(2,1)S(1)} %get-tuple-element.31), channel_id=1, source_target_pairs={{1,2},{2,1},{3,4},{4,3},{5,6},{6,5},{7,8},{8,7},{9,10},{10,9},{11,... | collective-permute-start | bytes 393224 | tf_op jit(solution)/shard_map/ppermute | solution.py:53
  48.4 8.6 %collective-permute-start.5 = (bf16[4,2,64,128]{3,2,1,0:T(8,128)(2,1)S(1)}, bf16[4,2,64,128]{3,2,1,0:T(8,128)(2,1)S(1)}, u32[]{:S(2)}, u32[]{:S(2)}) collective-permute-start(bf16[4,2,64,128]{3,2,1,0:T(8,128)(2,1)S(1)} %get-tuple-element.32), channel_id=1, source_target_pairs={{0,1},{1,0},{2,3},{3,2},{4,5},{5,4},{6,7},{7,6},{8,9},{9,8},{10,11... | collective-permute-start | bytes 393224 | tf_op jit(solution)/shard_map/ppermute | solution.py:53
  50.3 9.0 %collective-permute-start.6 = (bf16[4,2,64,128]{3,2,1,0:T(8,128)(2,1)S(1)}, bf16[4,2,64,128]{3,2,1,0:T(8,128)(2,1)S(1)}, u32[]{:S(2)}, u32[]{:S(2)}) collective-permute-start(bf16[4,2,64,128]{3,2,1,0:T(8,128)(2,1)S(1)} %get-tuple-element.33), channel_id=1, source_target_pairs={{1,2},{2,1},{3,4},{4,3},{5,6},{6,5},{7,8},{8,7},{9,10},{10,9},{11,... | collective-permute-start | bytes 393224 | tf_op jit(solution)/shard_map/ppermute | solution.py:53
  59.5 16.5 %collective-permute-start.7 = (bf16[4,64,128]{2,1,0:T(8,128)(2,1)S(1)}, bf16[4,64,128]{2,1,0:T(8,128)(2,1)S(1)}, u32[]{:S(2)}, u32[]{:S(2)}) collective-permute-start(bf16[4,64,128]{2,1,0:T(8,128)(2,1)S(1)} %get-tuple-element.35), channel_id=1, source_target_pairs={{0,32},{32,0},{64,96},{96,64},{128,160},{160,128},{192,224},{224,1... | collective-permute-start | bytes 196616 | tf_op jit(solution)/shard_map/ppermute | solution.py:44
  64.8 11.2 %collective-permute-start.8 = (bf16[4,64,128]{2,1,0:T(8,128)(2,1)S(1)}, bf16[4,64,128]{2,1,0:T(8,128)(2,1)S(1)}, u32[]{:S(2)}, u32[]{:S(2)}) collective-permute-start(bf16[4,64,128]{2,1,0:T(8,128)(2,1)S(1)} %get-tuple-element.36), channel_id=1, source_target_pairs={{0,64},{32,96},{64,0},{96,32},{128,192},{160,224},{192,128},{224,1... | collective-permute-start | bytes 196616 | tf_op jit(solution)/shard_map/ppermute | solution.py:44
  66.8 9.2 %collective-permute-start.9 = (bf16[4,64,128]{2,1,0:T(8,128)(2,1)S(1)}, bf16[4,64,128]{2,1,0:T(8,128)(2,1)S(1)}, u32[]{:S(2)}, u32[]{:S(2)}) collective-permute-start(bf16[4,64,128]{2,1,0:T(8,128)(2,1)S(1)} %get-tuple-element.37), channel_id=1, source_target_pairs={{0,96},{32,64},{64,32},{96,0},{128,224},{160,192},{192,160},{224,1... | collective-permute-start | bytes 196616 | tf_op jit(solution)/shard_map/ppermute | solution.py:44
